TPU v7x, 32 devices: a whole 2x2x4 slice. The times are simulated.
32 devices in a mesh: lon: 4 (over y, x), lat: 8 (over z, core).
Axes of the slice: x: 2, y: 2, z: 4, core: 2. Of those that a mesh axis runs over, the one named last changes fastest.
Arguments:
- wind_east: float32 [16, 64, 2048], P(None, 'lat', 'lon'), may hold values from -6 to 6
- wind_north: float32 [16, 64, 2048], P(None, 'lat', 'lon'), may hold values from -6 to 6
- potential_temp: float32 [16, 64, 2048], P(None, 'lat', 'lon'), may hold values from -6 to 6
- pressure: float32 [16, 64, 2048], P(None, 'lat', 'lon'), may hold values from -6 to 6
- moisture: float32 [16, 64, 2048], P(None, 'lat', 'lon'), may hold values from -6 to 6
- map_factor: float32 [64], P('lat'), may hold values from 1 to 4
- filter_rows: int32 [32], replicated, may hold values from 0 to 63, as said below
- filter_cutoff: int32 [32], replicated, may hold values from 1 to 1025, as said below
Outputs:
- new_east: float32 [16, 64, 2048], P(None, 'lat', 'lon')
- new_north: float32 [16, 64, 2048], P(None, 'lat', 'lon')
- new_temp: float32 [16, 64, 2048], P(None, 'lat', 'lon')
- new_pressure: float32 [16, 64, 2048], P(None, 'lat', 'lon')
- new_moisture: float32 [16, 64, 2048], P(None, 'lat', 'lon')
Inputs may be any that keep to these rules, and one draw needn't show every extreme that they name: `filter_rows`: ascending and without repeats; the rows are the first m and the last 32 - m latitude rows, for some m with 1 <= m <= 31. `filter_cutoff`: within each polar cap the count does not fall with the row's distance from the nearer pole; the row farthest from the pole in each cap keeps 1025.
All inputs are finite; a program needn't handle non-finite values.
Results may differ from a plain program's by a relative error of at most 0.000073.
Values sent between devices are 32-bit elements; how exact they have to be, the bound alone decides.
No kernel may reach another device: no remote copies, remote signals or barrier semaphores. Data moves between devices by JAX's collectives and lax.ppermute only.
A program may use at most 128 MiB of HBM per device.

v0:
```python
import math
import jax
import jax.numpy as jnp
from jax import lax
from jax.sharding import PartitionSpec as P

SUBSTEPS = 4
ADV_COEF = 0.1
SOUND = 0.4
THETA_DIV = 0.3


def extended_2(array, sides, width, wrap):
    for axis, dim in sides:
        devices, length = (lax.axis_size(axis), array.shape[dim])
        up = [(i, (i + 1) % devices) for i in range(devices if wrap else devices - 1)]
        down = [(j, i) for i, j in up]
        last = lax.slice_in_dim(array, length - width, length, axis=dim)
        initial = lax.slice_in_dim(array, 0, width, axis=dim)
        before = lax.ppermute(last, axis, up)
        after = lax.ppermute(initial, axis, down)
        array = jnp.concatenate([before, array, after], axis=dim)
    return array


def centred(shifted):
    return (
        shifted[0]
        - 9.0 * shifted[1]
        + 45.0 * shifted[2]
        - 45.0 * shifted[3]
        + 9.0 * shifted[4]
        - shifted[5]
    ) / 60.0


def damping(shifted, centre):
    return (
        shifted[0]
        - 6.0 * shifted[1]
        + 15.0 * shifted[2]
        - 20.0 * centre
        + 15.0 * shifted[3]
        - 6.0 * shifted[4]
        + shifted[5]
    ) / 60.0


def wave_table(circle):
    half = circle // 2
    points = jnp.arange(circle, dtype=jnp.int32)
    cos_waves = jnp.arange(half + 1, dtype=jnp.int32)
    sin_waves = jnp.arange(1, half, dtype=jnp.int32)
    cos_angles = (points[:, None] * cos_waves[None, :] % circle).astype(jnp.float32) * (
        2.0 * math.pi / circle
    )
    sin_angles = (points[:, None] * sin_waves[None, :] % circle).astype(jnp.float32) * (
        2.0 * math.pi / circle
    )
    table = jnp.concatenate([jnp.cos(cos_angles), jnp.sin(sin_angles)], axis=1)
    wave_index = jnp.concatenate([cos_waves, sin_waves])
    return (table, wave_index)


def filter_circles(circles, table, wave_index, item_cut, flagged, circle):
    spectra = jnp.dot(circles, table, precision=lax.Precision.HIGHEST)
    single = (wave_index == 0) | (wave_index == circle // 2)
    weights = jnp.where(single, 1.0, 2.0) / circle
    kept_mask = wave_index[None, :] < item_cut[:, None]
    spectra = jnp.where(kept_mask, spectra * weights[None, :], 0.0)
    smooth = lax.dot_general(
        spectra, table, (((1,), (1,)), ((), ())), precision=lax.Precision.HIGHEST
    )
    return jnp.where(flagged[:, None], smooth, circles)


def item_tables(item_rows, row_cut, row_flag, rows_dev):
    picked = item_rows[:, None] == jnp.arange(rows_dev, dtype=jnp.int32)[None, :]
    item_cut = jnp.sum(jnp.where(picked, row_cut[None, :], 0), axis=1)
    flagged = jnp.any(picked & row_flag[None, :], axis=1)
    return (item_cut, flagged)


def pole_mask(extended, lat_place, rows_dev, total_rows, depth, row_dim):
    ext_rows = lat_place * rows_dev - depth + jnp.arange(rows_dev + 2 * depth, dtype=jnp.int32)
    inside = (ext_rows >= 0) & (ext_rows < total_rows)
    shape_mask = [1] * extended.ndim
    shape_mask[row_dim] = rows_dev + 2 * depth
    return jnp.where(inside.reshape(shape_mask), extended, 0.0)


def shards(
    wind_east,
    wind_north,
    potential_temp,
    pressure,
    moisture,
    map_factor,
    filter_rows,
    filter_cutoff,
):
    levels, rows_dev, cols_dev = wind_east.shape
    lon_count = lax.axis_size("lon")
    lat_count = lax.axis_size("lat")
    lon_place = lax.axis_index("lon")
    lat_place = lax.axis_index("lat")
    circle = cols_dev * lon_count
    total_rows = rows_dev * lat_count
    local_rows = lat_place * rows_dev + jnp.arange(rows_dev, dtype=jnp.int32)
    matches = filter_rows[:, None] == local_rows[None, :]
    row_flag = jnp.any(matches, axis=0)
    row_cut = jnp.sum(jnp.where(matches, filter_cutoff[:, None], 0), axis=0)
    table, wave_index = wave_table(circle)
    stacked = jnp.stack([wind_east, wind_north, potential_temp, pressure, moisture])
    per_dev = levels * rows_dev // lon_count
    item_ids = lon_place * per_dev + jnp.arange(per_dev, dtype=jnp.int32)
    item_cut, flagged = item_tables(item_ids % rows_dev, row_cut, row_flag, rows_dev)
    results = []
    for field_index in range(5):
        blocks = stacked[field_index].reshape(lon_count, per_dev, cols_dev)
        circles = lax.all_to_all(blocks, "lon", split_axis=0, concat_axis=2, tiled=True)[0]
        smooth = filter_circles(circles, table, wave_index, item_cut, flagged, circle)
        returned = lax.all_to_all(smooth[None], "lon", split_axis=2, concat_axis=0, tiled=True)
        results.append(returned.reshape(levels, rows_dev, cols_dev))
    stacked = jnp.stack(results)
    extended = extended_2(stacked, (("lon", 3), ("lat", 2)), 3, True)
    extended = pole_mask(extended, lat_place, rows_dev, total_rows, 3, 2)
    along = [
        extended[:, :, 3 : 3 + rows_dev, 3 + offset : 3 + offset + cols_dev]
        for offset in (3, 2, 1, -1, -2, -3)
    ]
    across = [
        extended[:, :, 3 + offset : 3 + offset + rows_dev, 3 : 3 + cols_dev]
        for offset in (3, 2, 1, -1, -2, -3)
    ]
    east_wind = stacked[0]
    north_wind = stacked[1]
    coef_x = (ADV_COEF * map_factor)[:, None]
    zonal = east_wind[None] * centred(along) - jnp.abs(east_wind[None]) * damping(along, stacked)
    meridional = north_wind[None] * centred(across) - jnp.abs(north_wind[None]) * damping(
        across, stacked
    )
    tendency = -coef_x * zonal - ADV_COEF * meridional
    tend_east, tend_north, tend_temp, tend_press, tend_moist = (
        tendency[0],
        tendency[1],
        tendency[2],
        tendency[3],
        tendency[4],
    )
    theta_now = stacked[2]
    press_now = stacked[3]
    moist_now = stacked[4]
    grad_x = (SOUND * map_factor)[:, None]
    latitude = -0.5 * math.pi + (local_rows.astype(jnp.float32) + 0.5) * (math.pi / total_rows)
    coriolis = (0.5 * jnp.sin(latitude))[:, None]
    substep_dt = 1.0 / SUBSTEPS
    for substep in range(SUBSTEPS):
        press_ext = extended_2(press_now, (("lon", 2), ("lat", 1)), 1, True)
        press_ext = pole_mask(press_ext, lat_place, rows_dev, total_rows, 1, 1)
        press_dx = (press_ext[:, 1:-1, 2:] - press_ext[:, 1:-1, :-2]) * 0.5
        press_dy = (press_ext[:, 2:, 1:-1] - press_ext[:, :-2, 1:-1]) * 0.5
        east_wind = east_wind + substep_dt * (tend_east - grad_x * press_dx + coriolis * north_wind)
        north_wind = north_wind + substep_dt * (
            tend_north - SOUND * press_dy - coriolis * east_wind
        )
        east_ext = extended_2(east_wind, (("lon", 2),), 1, True)
        north_ext = extended_2(north_wind, (("lat", 1),), 1, False)
        diverge = (
            grad_x * (east_ext[:, :, 2:] - east_ext[:, :, :-2]) * 0.5
            + SOUND * (north_ext[:, 2:, :] - north_ext[:, :-2, :]) * 0.5
        )
        press_now = press_now + substep_dt * (tend_press - diverge)
        theta_now = theta_now + substep_dt * (tend_temp - THETA_DIV * diverge)
        moist_now = moist_now + substep_dt * tend_moist
    return (east_wind, north_wind, theta_now, press_now, moist_now)


def solution(mesh):
    in_specs = (
        P(None, "lat", "lon"),
        P(None, "lat", "lon"),
        P(None, "lat", "lon"),
        P(None, "lat", "lon"),
        P(None, "lat", "lon"),
        P("lat"),
        P(),
        P(),
    )
    out_specs = (
        P(None, "lat", "lon"),
        P(None, "lat", "lon"),
        P(None, "lat", "lon"),
        P(None, "lat", "lon"),
        P(None, "lat", "lon"),
    )
    return jax.shard_map(shards, mesh=mesh, in_specs=in_specs, out_specs=out_specs, check_vma=False)
```

profile of v0, /device:TPU:0, one launch (start us, length us, event | category | flops | bytes accessed | tf_op | source)
XLA Modules:
  0.0 494.1 jit_solution(3201918005113495006)
XLA Ops:
  0.6 5.2 %all-to-all-start = ((f32[4,32,512]{2,1,0:T(8,128)}), f32[4,32,512]{2,1,0:T(8,128)S(1)}, u32[]{:S(2)}, u32[]{:S(2)}) async-start(f32[4,32,512]{2,1,0:T(8,128)} %bitcast.201), calls=%async_computation | async-start | bytes 524288 | tf_op jit(solution)/shard_map/all_to_all | solution.py:121
  5.9 35.4 %fusion.3 = f32[2048,1025]{1,0:T(8,128)} fusion(), kind=kLoop, calls=%fused_computation.10 | loop fusion | flops 29388800 | bytes 8396800 | tf_op jit(solution)/shard_map/cos | solution.py:60
  41.7 32.0 %fusion.10 = f32[2048,1023]{1,0:T(8,128)} fusion(s32[1023]{0:T(1024)S(1)} %iota_add_fusion), kind=kLoop, calls=%fused_computation.17 | loop fusion | flops 29331456 | bytes 8384508 | tf_op jit(solution)/shard_map/sin | solution.py:60
  73.9 4.2 all-to-all-start.4
  78.2 5.3 %all-to-all-done.4 = f32[4,32,512]{2,1,0:T(8,128)S(1)} async-done(((f32[4,32,512]{2,1,0:T(8,128)}), f32[4,32,512]{2,1,0:T(8,128)S(1)}, u32[]{:S(2)}, u32[]{:S(2)}) %all-to-all-start.4) | async-done | bytes 262176 | tf_op jit(solution)/shard_map/all_to_all | solution.py:121
  83.5 3.4 all-to-all-start.8
  87.5 4.8 all-to-all-done.8
  92.2 3.7 all-to-all-start.6
  96.3 17.9 %fusion.26 = f32[32,2048]{1,0:T(8,128)} fusion(f32[32,2048]{1,0:T(8,128)S(1)} %bitcast.182, f32[2048]{0:T(1024)S(1)} %get-tuple-element.18, s32[2048]{0:T(1024)S(1)} %get-tuple-element.19, s32[32]{0:T(128)S(1)} %select_reduce_fusion, f32[2048,1023]{1,0:T(8,128)} %fusion.10, f32[2048,1025]{1,0:T(8,128)} %fusion.3), kind=kOutput, calls=%fused_computation.44 | convolution fusion | flops 1615003648 | bytes 17318016 | tf_op jit(solution)/shard_map/dot_general | solution.py:66
  114.2 15.2 %fusion.28 = f32[32,2048]{1,0:T(8,128)} fusion(f32[32,2048]{1,0:T(8,128)S(1)} %bitcast.184, f32[2048]{0:T(1024)S(1)} %get-tuple-element.18, s32[2048]{0:T(1024)S(1)} %get-tuple-element.19, s32[32]{0:T(128)S(1)} %select_reduce_fusion, f32[2048,1023]{1,0:T(8,128)} %fusion.10, f32[2048,1025]{1,0:T(8,128)S(1)} %bitcast.148), kind=kOutput, calls=%fused_computation.46 | convolution fusion | flops 1615003648 | bytes 17318016 | tf_op jit(solution)/shard_map/dot_general | solution.py:66
  129.4 16.1 %fusion.18 = f32[1,32,2048]{2,1,0:T(8,128)S(1)} fusion(f32[32,2048]{1,0:T(8,128)S(1)} %bitcast.183, f32[32,2048]{1,0:T(8,128)} %fusion.26, pred[32]{0:T(512)(128)(4,1)S(1)} %fusion.96, f32[2048,1023]{1,0:T(8,128)S(1)} %bitcast.150, f32[2048,1025]{1,0:T(8,128)S(1)} %bitcast.148), kind=kOutput, calls=%fused_computation.31 | convolution fusion | flops 1614872576 | bytes 17563680 | tf_op jit(solution)/shard_map/dot_general | solution.py:71
  145.5 16.3 %fusion.14 = f32[1,32,2048]{2,1,0:T(8,128)S(1)} fusion(f32[32,2048]{1,0:T(8,128)S(1)} %bitcast.185, f32[32,2048]{1,0:T(8,128)} %fusion.28, pred[32]{0:T(512)(128)(4,1)S(1)} %fusion.96, f32[2048,1023]{1,0:T(8,128)S(1)} %bitcast.150, f32[2048,1025]{1,0:T(8,128)S(1)} %bitcast.148), kind=kOutput, calls=%fused_computation.23 | convolution fusion | flops 1614872576 | bytes 17563680 | tf_op jit(solution)/shard_map/dot_general | solution.py:71
  161.8 11.5 %fusion.24 = f32[32,2048]{1,0:T(8,128)} fusion(f32[32,2048]{1,0:T(8,128)S(1)} %bitcast.178, f32[2048]{0:T(1024)S(1)} %get-tuple-element.18, s32[2048]{0:T(1024)S(1)} %get-tuple-element.19, s32[32]{0:T(128)S(1)} %select_reduce_fusion, f32[2048,1023]{1,0:T(8,128)S(1)} %bitcast.150, f32[2048,1025]{1,0:T(8,128)S(1)} %bitcast.148), kind=kOutput, calls=%fused_computation.42 | convolution fusion | flops 1615003648 | bytes 17318016 | tf_op jit(solution)/shard_map/dot_general | solution.py:66
  173.3 4.6 all-to-all-start.2
  177.9 20.0 %fusion.22 = f32[1,32,2048]{2,1,0:T(8,128)S(1)} fusion(f32[32,2048]{1,0:T(8,128)S(1)} %bitcast.179, f32[32,2048]{1,0:T(8,128)} %fusion.24, pred[32]{0:T(512)(128)(4,1)S(1)} %fusion.96, f32[2048,1023]{1,0:T(8,128)} %fusion.10, f32[2048,1025]{1,0:T(8,128)} %fusion.3), kind=kOutput, calls=%fused_computation.39 | convolution fusion | flops 1614872576 | bytes 17563680 | tf_op jit(solution)/shard_map/dot_general | solution.py:71
  199.2 9.3 %reduce.4 = f32[2048,32]{1,0:T(8,128)S(1)} reduce(f32[2048,1,32]{2,1,0:T(1,128)S(1)} %bitcast.156, f32[]{:T(128)} %broadcast.311), dimensions={1}, to_apply=%bitcast.123.reduce_sub_computation | reduce | bytes 524292
  210.4 4.4 all-to-all-start.1
  214.8 15.9 %fusion.27 = f32[32,2048]{1,0:T(8,128)} fusion(f32[32,2048]{1,0:T(8,128)S(1)} %bitcast.180, f32[2048]{0:T(1024)S(1)} %get-tuple-element.18, s32[2048]{0:T(1024)S(1)} %get-tuple-element.19, s32[32]{0:T(128)S(1)} %select_reduce_fusion, f32[2048,1023]{1,0:T(8,128)} %fusion.10, f32[2048,1025]{1,0:T(8,128)} %fusion.3), kind=kOutput, calls=%fused_computation.45 | convolution fusion | flops 1615003648 | bytes 17318016 | tf_op jit(solution)/shard_map/dot_general | solution.py:66
  231.2 9.3 %reduce.8 = f32[2048,32]{1,0:T(8,128)S(1)} reduce(f32[2048,1,32]{2,1,0:T(1,128)S(1)} %bitcast.157, f32[]{:T(128)} %broadcast.311), dimensions={1}, to_apply=%bitcast.131.reduce_sub_computation | reduce | bytes 524292
  241.8 4.4 all-to-all-start.9
  246.2 20.0 %fusion.16 = f32[1,32,2048]{2,1,0:T(8,128)S(1)} fusion(f32[32,2048]{1,0:T(8,128)S(1)} %bitcast.181, f32[32,2048]{1,0:T(8,128)} %fusion.27, pred[32]{0:T(512)(128)(4,1)S(1)} %fusion.96, f32[2048,1023]{1,0:T(8,128)} %fusion.10, f32[2048,1025]{1,0:T(8,128)} %fusion.3), kind=kOutput, calls=%fused_computation.27 | convolution fusion | flops 1614872576 | bytes 17563680 | tf_op jit(solution)/shard_map/dot_general | solution.py:71
  267.0 9.3 %reduce.2 = f32[2048,32]{1,0:T(8,128)S(1)} reduce(f32[2048,1,32]{2,1,0:T(1,128)S(1)} %bitcast.158, f32[]{:T(128)} %broadcast.311), dimensions={1}, to_apply=%bitcast.125.reduce_sub_computation | reduce | bytes 524292
  277.6 4.6 all-to-all-start.7
  282.2 15.9 %fusion.25 = f32[32,2048]{1,0:T(8,128)} fusion(f32[32,2048]{1,0:T(8,128)S(1)} %bitcast.176, f32[2048]{0:T(1024)S(1)} %get-tuple-element.18, s32[2048]{0:T(1024)S(1)} %get-tuple-element.19, s32[32]{0:T(128)S(1)} %select_reduce_fusion, f32[2048,1023]{1,0:T(8,128)} %fusion.10, f32[2048,1025]{1,0:T(8,128)} %fusion.3), kind=kOutput, calls=%fused_computation.43 | convolution fusion | flops 1615003648 | bytes 17318016 | tf_op jit(solution)/shard_map/dot_general | solution.py:66
  298.6 9.3 %reduce.6 = f32[2048,32]{1,0:T(8,128)S(1)} reduce(f32[2048,1,32]{2,1,0:T(1,128)S(1)} %bitcast.159, f32[]{:T(128)} %broadcast.311), dimensions={1}, to_apply=%bitcast.129.reduce_sub_computation | reduce | bytes 524292
  309.1 4.4 all-to-all-start.5
  313.5 20.0 %fusion.20 = f32[1,32,2048]{2,1,0:T(8,128)S(1)} fusion(f32[32,2048]{1,0:T(8,128)S(1)} %bitcast.177, f32[32,2048]{1,0:T(8,128)} %fusion.25, pred[32]{0:T(512)(128)(4,1)S(1)} %fusion.96, f32[2048,1023]{1,0:T(8,128)} %fusion.10, f32[2048,1025]{1,0:T(8,128)} %fusion.3), kind=kOutput, calls=%fused_computation.35 | convolution fusion | flops 1614872576 | bytes 17563680 | tf_op jit(solution)/shard_map/dot_general | solution.py:71
  334.0 9.6 %reduce = f32[2048,32]{1,0:T(8,128)S(1)} reduce(f32[2048,1,32]{2,1,0:T(1,128)S(1)} %bitcast.160, f32[]{:T(128)} %broadcast.311), dimensions={1}, to_apply=%bitcast.127.reduce_sub_computation | reduce | bytes 524292
  346.1 1.6 reshape.129
  354.9 4.2 all-to-all-start.3
  359.2 2.0 collective-permute-start.4
  370.8 1.9 collective-permute-start.1
  373.0 3.5 collective-permute-start.7
  377.7 4.0 collective-permute-done.1
  383.6 12.2 %collective-permute-done.3 = f32[5,16,3,518]{3,1,2,0:T(8,128)S(1)} collective-permute-done((f32[5,16,3,518]{3,1,2,0:T(8,128)S(1)}, f32[5,16,3,518]{3,1,2,0:T(8,128)S(1)}, u32[]{:S(2)}, u32[]{:S(2)}) %collective-permute-start.3) | collective-permute-done | bytes 497312 | tf_op jit(solution)/shard_map/ppermute | solution.py:21
  396.2 4.4 collective-permute-done.2
  402.3 4.2 multiply_subtract_fusion
  408.2 3.2 collective-permute-start.11
  413.5 2.7 collective-permute-done.8
  418.2 2.4 collective-permute-start.13
  420.5 2.2 collective-permute-done.12
  423.8 3.5 collective-permute-start.15
  427.4 2.1 collective-permute-done.14
  431.4 3.0 collective-permute-start.19
  434.5 2.2 collective-permute-start.16
  436.9 2.2 collective-permute-done.16
  439.1 2.9 collective-permute-done.17
  442.8 2.5 collective-permute-start.21
  445.3 2.2 collective-permute-done.20
  448.5 3.5 collective-permute-start.23
  452.1 1.7 collective-permute-done.22
  455.7 3.0 collective-permute-start.27
  458.9 2.2 collective-permute-start.24
  461.2 2.2 collective-permute-done.24
  463.4 2.9 collective-permute-done.25
  467.8 2.5 collective-permute-start.29
  470.3 2.2 collective-permute-done.28
  473.6 3.5 collective-permute-start.31
  477.1 1.7 collective-permute-done.30
  480.8 3.0 collective-permute-start.35
  483.9 2.2 collective-permute-start.32
  486.2 2.2 collective-permute-done.32
  488.4 2.9 collective-permute-done.33
  492.3 1.6 multiply_add_fusion.1
  (169 shorter events, 53.8 us)
Async XLA Ops:
  0.6 73.3 %all-to-all-start = ((f32[4,32,512]{2,1,0:T(8,128)}), f32[4,32,512]{2,1,0:T(8,128)S(1)}, u32[]{:S(2)}, u32[]{:S(2)}) async-start(f32[4,32,512]{2,1,0:T(8,128)} %bitcast.201), calls=%async_computation | async-start | bytes 524288 | tf_op jit(solution)/shard_map/all_to_all | solution.py:121
  5.9 35.5 %copy-start.5 = (s32[32]{0:T(128)S(1)}, s32[32]{0:T(128)}, u32[]{:S(2)}) copy-start(s32[32]{0:T(128)} %param.14) | copy-start | bytes 388
  5.9 35.6 %copy-start.4 = (s32[32]{0:T(128)S(1)}, s32[32]{0:T(128)}, u32[]{:S(2)}) copy-start(s32[32]{0:T(128)} %param.15) | copy-start | bytes 388
  41.7 45.2 %copy-start.6 = (f32[8]{0:T(128)S(1)}, f32[8]{0:T(128)}, u32[]{:S(2)}) copy-start(f32[8]{0:T(128)} %param.13) | copy-start | bytes 100
  73.9 9.6 %all-to-all-start.4 = ((f32[4,32,512]{2,1,0:T(8,128)}), f32[4,32,512]{2,1,0:T(8,128)S(1)}, u32[]{:S(2)}, u32[]{:S(2)}) async-start(f32[4,32,512]{2,1,0:T(8,128)} %bitcast.17), calls=%async_computation.4 | async-start | bytes 524288 | tf_op jit(solution)/shard_map/all_to_all | solution.py:121
  83.5 8.8 %all-to-all-start.8 = ((f32[4,32,512]{2,1,0:T(8,128)}), f32[4,32,512]{2,1,0:T(8,128)S(1)}, u32[]{:S(2)}, u32[]{:S(2)}) async-start(f32[4,32,512]{2,1,0:T(8,128)} %bitcast.33), calls=%async_computation.8 | async-start | bytes 524288 | tf_op jit(solution)/shard_map/all_to_all | solution.py:121
  92.2 81.1 %all-to-all-start.6 = ((f32[4,32,512]{2,1,0:T(8,128)}), f32[4,32,512]{2,1,0:T(8,128)S(1)}, u32[]{:S(2)}, u32[]{:S(2)}) async-start(f32[4,32,512]{2,1,0:T(8,128)} %bitcast.25), calls=%async_computation.6 | async-start | bytes 524288 | tf_op jit(solution)/shard_map/all_to_all | solution.py:121
  96.1 18.0 %slice-start = ((s8[9437184]{0:T(1024)(128)(4,1)}), s8[4194304]{0:T(1024)(128)(4,1)S(1)}, s32[]{:S(2)}) async-start(s8[9437184]{0:T(1024)(128)(4,1)} %bitcast.147), calls=%async_computation.10 | async-start | bytes 8388608
  96.2 17.9 %slice-start.1 = ((s8[9437184]{0:T(1024)(128)(4,1)}), s8[4194304]{0:T(1024)(128)(4,1)S(1)}, s32[]{:S(2)}) async-start(s8[9437184]{0:T(1024)(128)(4,1)} %bitcast.147), calls=%async_computation.11 | async-start | bytes 8388608
  96.2 17.9 %slice-start.2 = ((s8[9437184]{0:T(1024)(128)(4,1)}), s8[1048576]{0:T(1024)(128)(4,1)S(1)}, s32[]{:S(2)}) async-start(s8[9437184]{0:T(1024)(128)(4,1)} %bitcast.147), calls=%async_computation.12 | async-start | bytes 2097152
  96.3 33.1 %slice-start.3 = ((s8[8388608]{0:T(1024)(128)(4,1)}), s8[4194304]{0:T(1024)(128)(4,1)S(1)}, s32[]{:S(2)}) async-start(s8[8388608]{0:T(1024)(128)(4,1)} %bitcast.149), calls=%async_computation.13 | async-start | bytes 8388608
  114.2 15.2 %slice-start.4 = ((s8[8388608]{0:T(1024)(128)(4,1)}), s8[4194304]{0:T(1024)(128)(4,1)S(1)}, s32[]{:S(2)}) async-start(s8[8388608]{0:T(1024)(128)(4,1)} %bitcast.149), calls=%async_computation.14 | async-start | bytes 8388608
  173.3 36.4 %all-to-all-start.2 = ((f32[4,32,512]{2,1,0:T(8,128)}), f32[4,32,512]{2,1,0:T(8,128)S(1)}, u32[]{:S(2)}, u32[]{:S(2)}) async-start(f32[4,32,512]{2,1,0:T(8,128)} %bitcast.202), calls=%async_computation.2 | async-start | bytes 524288 | tf_op jit(solution)/shard_map/all_to_all | solution.py:121
  209.7 0.7 copy-start.2
  210.4 31.3 %all-to-all-start.1 = ((f32[4,1,16384]{2,1,0:T(1,128)}), f32[4,1,16384]{2,1,0:T(1,128)S(1)}, u32[]{:S(2)}, u32[]{:S(2)}) async-start(f32[4,1,16384]{2,1,0:T(1,128)} %reshape.128), calls=%async_computation.1 | async-start | bytes 524288 | tf_op jit(solution)/shard_map/all_to_all | solution.py:123
  241.8 35.8 %all-to-all-start.9 = ((f32[4,1,16384]{2,1,0:T(1,128)}), f32[4,1,16384]{2,1,0:T(1,128)S(1)}, u32[]{:S(2)}, u32[]{:S(2)}) async-start(f32[4,1,16384]{2,1,0:T(1,128)} %reshape.136), calls=%async_computation.9 | async-start | bytes 524288 | tf_op jit(solution)/shard_map/all_to_all | solution.py:123
  246.2 20.0 %copy-start.3 = (f32[4,32,512]{2,1,0:T(8,128)S(1)}, f32[4,32,512]{2,1,0:T(8,128)}, u32[]{:S(2)}) copy-start(f32[4,32,512]{2,1,0:T(8,128)} %copy-done.2) | copy-start | bytes 786436
  277.6 31.5 %all-to-all-start.7 = ((f32[4,1,16384]{2,1,0:T(1,128)}), f32[4,1,16384]{2,1,0:T(1,128)S(1)}, u32[]{:S(2)}, u32[]{:S(2)}) async-start(f32[4,1,16384]{2,1,0:T(1,128)} %reshape.130), calls=%async_computation.7 | async-start | bytes 524288 | tf_op jit(solution)/shard_map/all_to_all | solution.py:123
  309.1 45.8 %all-to-all-start.5 = ((f32[4,1,16384]{2,1,0:T(1,128)}), f32[4,1,16384]{2,1,0:T(1,128)S(1)}, u32[]{:S(2)}, u32[]{:S(2)}) async-start(f32[4,1,16384]{2,1,0:T(1,128)} %reshape.134), calls=%async_computation.5 | async-start | bytes 524288 | tf_op jit(solution)/shard_map/all_to_all | solution.py:123
  354.9 11.1 %all-to-all-start.3 = ((f32[4,1,16384]{2,1,0:T(1,128)}), f32[4,1,16384]{2,1,0:T(1,128)S(1)}, u32[]{:S(2)}, u32[]{:S(2)}) async-start(f32[4,1,16384]{2,1,0:T(1,128)} %reshape.132), calls=%async_computation.3 | async-start | bytes 524288 | tf_op jit(solution)/shard_map/all_to_all | solution.py:123
  359.2 13.5 %collective-permute-start.4 = (f32[16,8,1]{2,1,0:T(8,128)S(1)}, f32[16,8,1]{2,1,0:T(8,128)S(1)}, u32[]{:S(2)}, u32[]{:S(2)}) collective-permute-start(f32[16,8,1]{2,1,0:T(8,128)S(1)} %get-tuple-element.60), channel_id=1, source_target_pairs={{0,8},{8,16},{16,24},{24,0},{1,9},{9,17},{17,25},{25,1},{2,10},{10... | collective-permute-start | bytes 1544 | tf_op jit(solution)/shard_map/ppermute | solution.py:20
  361.2 11.4 %collective-permute-start.5 = (f32[16,8,1]{2,1,0:T(8,128)S(1)}, f32[16,8,1]{2,1,0:T(8,128)S(1)}, u32[]{:S(2)}, u32[]{:S(2)}) collective-permute-start(f32[16,8,1]{2,1,0:T(8,128)S(1)} %get-tuple-element.61), channel_id=1, source_target_pairs={{8,0},{16,8},{24,16},{0,24},{9,1},{17,9},{25,17},{1,25},{10,2},{18... | collective-permute-start | bytes 1544 | tf_op jit(solution)/shard_map/ppermute | solution.py:21
  369.7 8.0 %collective-permute-start = (f32[5,16,8,3]{3,2,1,0:T(8,128)S(1)}, f32[5,16,8,3]{3,2,1,0:T(8,128)S(1)}, u32[]{:S(2)}, u32[]{:S(2)}) collective-permute-start(f32[5,16,8,3]{3,2,1,0:T(8,128)S(1)} %get-tuple-element.24), channel_id=1, source_target_pairs={{0,8},{8,16},{16,24},{24,0},{1,9},{9,17},{17,25},{25,1},{2,10},{10... | collective-permute-start | bytes 23048 | tf_op jit(solution)/shard_map/ppermute | solution.py:20
  370.8 10.9 %collective-permute-start.1 = (f32[5,16,8,3]{3,2,1,0:T(8,128)S(1)}, f32[5,16,8,3]{3,2,1,0:T(8,128)S(1)}, u32[]{:S(2)}, u32[]{:S(2)}) collective-permute-start(f32[5,16,8,3]{3,2,1,0:T(8,128)S(1)} %get-tuple-element.25), channel_id=1, source_target_pairs={{8,0},{16,8},{24,16},{0,24},{9,1},{17,9},{25,17},{1,25},{10,2},{18... | collective-permute-start | bytes 23048 | tf_op jit(solution)/shard_map/ppermute | solution.py:21
  372.9 10.4 %collective-permute-start.6 = (f32[16,1,514]{2,1,0:T(1,128)S(1)}, f32[16,1,514]{2,1,0:T(1,128)S(1)}, u32[]{:S(2)}, u32[]{:S(2)}) collective-permute-start(f32[16,1,514]{2,1,0:T(1,128)S(1)} %get-tuple-element.32), channel_id=1, source_target_pairs={{0,1},{1,2},{2,3},{3,4},{4,5},{5,6},{6,7},{7,0},{8,9},{9,10},{10,1... | collective-permute-start | bytes 98696 | tf_op jit(solution)/shard_map/ppermute | solution.py:20
  373.0 10.3 %collective-permute-start.7 = (f32[16,1,514]{2,1,0:T(1,128)S(1)}, f32[16,1,514]{2,1,0:T(1,128)S(1)}, u32[]{:S(2)}, u32[]{:S(2)}) collective-permute-start(f32[16,1,514]{2,1,0:T(1,128)S(1)} %get-tuple-element.33), channel_id=1, source_target_pairs={{1,0},{2,1},{3,2},{4,3},{5,4},{6,5},{7,6},{0,7},{9,8},{10,9},{11,1... | collective-permute-start | bytes 98696 | tf_op jit(solution)/shard_map/ppermute | solution.py:21
  382.6 13.2 %collective-permute-start.3 = (f32[5,16,3,518]{3,1,2,0:T(8,128)S(1)}, f32[5,16,3,518]{3,1,2,0:T(8,128)S(1)}, u32[]{:S(2)}, u32[]{:S(2)}) collective-permute-start(f32[5,16,3,518]{3,1,2,0:T(8,128)S(1)} %copy.108), channel_id=1, source_target_pairs={{1,0},{2,1},{3,2},{4,3},{5,4},{6,5},{7,6},{0,7},{9,8},{10,9},{11,1... | collective-permute-start | bytes 1491848 | tf_op jit(solution)/shard_map/ppermute | solution.py:21
  382.7 17.9 %collective-permute-start.2 = (f32[5,16,3,518]{3,1,2,0:T(8,128)S(1)}, f32[5,16,3,518]{3,1,2,0:T(8,128)S(1)}, u32[]{:S(2)}, u32[]{:S(2)}) collective-permute-start(f32[5,16,3,518]{3,1,2,0:T(8,128)S(1)} %copy.107), channel_id=1, source_target_pairs={{0,1},{1,2},{2,3},{3,4},{4,5},{5,6},{6,7},{7,0},{8,9},{9,10},{10,1... | collective-permute-start | bytes 1491848 | tf_op jit(solution)/shard_map/ppermute | solution.py:20
  406.9 10.3 %collective-permute-start.10 = (f32[16,1,512]{2,1,0:T(1,128)S(1)}, f32[16,1,512]{2,1,0:T(1,128)S(1)}, u32[]{:S(2)}, u32[]{:S(2)}) collective-permute-start(f32[16,1,512]{2,1,0:T(1,128)S(1)} %get-tuple-element.54), channel_id=1, source_target_pairs={{1,0},{2,1},{3,2},{4,3},{5,4},{6,5},{7,6},{9,8},{10,9},{11,10},{12... | collective-permute-start | bytes 98312 | tf_op jit(solution)/shard_map/ppermute | solution.py:21
  408.2 9.1 %collective-permute-start.11 = (f32[16,1,512]{2,1,0:T(1,128)S(1)}, f32[16,1,512]{2,1,0:T(1,128)S(1)}, u32[]{:S(2)}, u32[]{:S(2)}) collective-permute-start(f32[16,1,512]{2,1,0:T(1,128)S(1)} %get-tuple-element.55), channel_id=1, source_target_pairs={{0,1},{1,2},{2,3},{3,4},{4,5},{5,6},{6,7},{8,9},{9,10},{10,11},{11... | collective-permute-start | bytes 98312 | tf_op jit(solution)/shard_map/ppermute | solution.py:20
  411.5 4.8 collective-permute-start.8
  412.1 5.2 %collective-permute-start.9 = (f32[16,8,1]{2,1,0:T(8,128)S(1)}, f32[16,8,1]{2,1,0:T(8,128)S(1)}, u32[]{:S(2)}, u32[]{:S(2)}) collective-permute-start(f32[16,8,1]{2,1,0:T(8,128)S(1)} %get-tuple-element.53), channel_id=1, source_target_pairs={{0,8},{8,16},{16,24},{24,0},{1,9},{9,17},{17,25},{25,1},{2,10},{10... | collective-permute-start | bytes 1544 | tf_op jit(solution)/shard_map/ppermute | solution.py:20
  417.6 5.2 %collective-permute-start.12 = (f32[16,8,1]{2,1,0:T(8,128)S(1)}, f32[16,8,1]{2,1,0:T(8,128)S(1)}, u32[]{:S(2)}, u32[]{:S(2)}) collective-permute-start(f32[16,8,1]{2,1,0:T(8,128)S(1)} %get-tuple-element.50), channel_id=1, source_target_pairs={{0,8},{8,16},{16,24},{24,0},{1,9},{9,17},{17,25},{25,1},{2,10},{10... | collective-permute-start | bytes 1544 | tf_op jit(solution)/shard_map/ppermute | solution.py:20
  418.2 5.3 %collective-permute-start.13 = (f32[16,8,1]{2,1,0:T(8,128)S(1)}, f32[16,8,1]{2,1,0:T(8,128)S(1)}, u32[]{:S(2)}, u32[]{:S(2)}) collective-permute-start(f32[16,8,1]{2,1,0:T(8,128)S(1)} %get-tuple-element.51), channel_id=1, source_target_pairs={{8,0},{16,8},{24,16},{0,24},{9,1},{17,9},{25,17},{1,25},{10,2},{18... | collective-permute-start | bytes 1544 | tf_op jit(solution)/shard_map/ppermute | solution.py:21
  423.8 5.7 %collective-permute-start.14 = (f32[16,1,514]{2,1,0:T(1,128)S(1)}, f32[16,1,514]{2,1,0:T(1,128)S(1)}, u32[]{:S(2)}, u32[]{:S(2)}) collective-permute-start(f32[16,1,514]{2,1,0:T(1,128)S(1)} %get-tuple-element.30), channel_id=1, source_target_pairs={{0,1},{1,2},{2,3},{3,4},{4,5},{5,6},{6,7},{7,0},{8,9},{9,10},{10,1... | collective-permute-start | bytes 98696 | tf_op jit(solution)/shard_map/ppermute | solution.py:20
  423.8 5.6 %collective-permute-start.15 = (f32[16,1,514]{2,1,0:T(1,128)S(1)}, f32[16,1,514]{2,1,0:T(1,128)S(1)}, u32[]{:S(2)}, u32[]{:S(2)}) collective-permute-start(f32[16,1,514]{2,1,0:T(1,128)S(1)} %get-tuple-element.31), channel_id=1, source_target_pairs={{1,0},{2,1},{3,2},{4,3},{5,4},{6,5},{7,6},{0,7},{9,8},{10,9},{11,1... | collective-permute-start | bytes 98696 | tf_op jit(solution)/shard_map/ppermute | solution.py:21
  430.1 11.8 %collective-permute-start.18 = (f32[16,1,512]{2,1,0:T(1,128)S(1)}, f32[16,1,512]{2,1,0:T(1,128)S(1)}, u32[]{:S(2)}, u32[]{:S(2)}) collective-permute-start(f32[16,1,512]{2,1,0:T(1,128)S(1)} %get-tuple-element.48), channel_id=1, source_target_pairs={{1,0},{2,1},{3,2},{4,3},{5,4},{6,5},{7,6},{9,8},{10,9},{11,10},{12... | collective-permute-start | bytes 98312 | tf_op jit(solution)/shard_map/ppermute | solution.py:21
  431.4 10.5 %collective-permute-start.19 = (f32[16,1,512]{2,1,0:T(1,128)S(1)}, f32[16,1,512]{2,1,0:T(1,128)S(1)}, u32[]{:S(2)}, u32[]{:S(2)}) collective-permute-start(f32[16,1,512]{2,1,0:T(1,128)S(1)} %get-tuple-element.49), channel_id=1, source_target_pairs={{0,1},{1,2},{2,3},{3,4},{4,5},{5,6},{6,7},{8,9},{9,10},{10,11},{11... | collective-permute-start | bytes 98312 | tf_op jit(solution)/shard_map/ppermute | solution.py:20
  434.5 4.5 collective-permute-start.16
  436.8 5.2 %collective-permute-start.17 = (f32[16,8,1]{2,1,0:T(8,128)S(1)}, f32[16,8,1]{2,1,0:T(8,128)S(1)}, u32[]{:S(2)}, u32[]{:S(2)}) collective-permute-start(f32[16,8,1]{2,1,0:T(8,128)S(1)} %get-tuple-element.47), channel_id=1, source_target_pairs={{0,8},{8,16},{16,24},{24,0},{1,9},{9,17},{17,25},{25,1},{2,10},{10... | collective-permute-start | bytes 1544 | tf_op jit(solution)/shard_map/ppermute | solution.py:20
  442.3 5.2 %collective-permute-start.20 = (f32[16,8,1]{2,1,0:T(8,128)S(1)}, f32[16,8,1]{2,1,0:T(8,128)S(1)}, u32[]{:S(2)}, u32[]{:S(2)}) collective-permute-start(f32[16,8,1]{2,1,0:T(8,128)S(1)} %get-tuple-element.44), channel_id=1, source_target_pairs={{0,8},{8,16},{16,24},{24,0},{1,9},{9,17},{17,25},{25,1},{2,10},{10... | collective-permute-start | bytes 1544 | tf_op jit(solution)/shard_map/ppermute | solution.py:20
  442.8 5.4 %collective-permute-start.21 = (f32[16,8,1]{2,1,0:T(8,128)S(1)}, f32[16,8,1]{2,1,0:T(8,128)S(1)}, u32[]{:S(2)}, u32[]{:S(2)}) collective-permute-start(f32[16,8,1]{2,1,0:T(8,128)S(1)} %get-tuple-element.45), channel_id=1, source_target_pairs={{8,0},{16,8},{24,16},{0,24},{9,1},{17,9},{25,17},{1,25},{10,2},{18... | collective-permute-start | bytes 1544 | tf_op jit(solution)/shard_map/ppermute | solution.py:21
  448.5 5.3 %collective-permute-start.22 = (f32[16,1,514]{2,1,0:T(1,128)S(1)}, f32[16,1,514]{2,1,0:T(1,128)S(1)}, u32[]{:S(2)}, u32[]{:S(2)}) collective-permute-start(f32[16,1,514]{2,1,0:T(1,128)S(1)} %get-tuple-element.28), channel_id=1, source_target_pairs={{0,1},{1,2},{2,3},{3,4},{4,5},{5,6},{6,7},{7,0},{8,9},{9,10},{10,1... | collective-permute-start | bytes 98696 | tf_op jit(solution)/shard_map/ppermute | solution.py:20
  448.5 5.2 %collective-permute-start.23 = (f32[16,1,514]{2,1,0:T(1,128)S(1)}, f32[16,1,514]{2,1,0:T(1,128)S(1)}, u32[]{:S(2)}, u32[]{:S(2)}) collective-permute-start(f32[16,1,514]{2,1,0:T(1,128)S(1)} %get-tuple-element.29), channel_id=1, source_target_pairs={{1,0},{2,1},{3,2},{4,3},{5,4},{6,5},{7,6},{0,7},{9,8},{10,9},{11,1... | collective-permute-start | bytes 98696 | tf_op jit(solution)/shard_map/ppermute | solution.py:21
  454.4 11.8 %collective-permute-start.26 = (f32[16,1,512]{2,1,0:T(1,128)S(1)}, f32[16,1,512]{2,1,0:T(1,128)S(1)}, u32[]{:S(2)}, u32[]{:S(2)}) collective-permute-start(f32[16,1,512]{2,1,0:T(1,128)S(1)} %get-tuple-element.42), channel_id=1, source_target_pairs={{1,0},{2,1},{3,2},{4,3},{5,4},{6,5},{7,6},{9,8},{10,9},{11,10},{12... | collective-permute-start | bytes 98312 | tf_op jit(solution)/shard_map/ppermute | solution.py:21
  455.7 10.5 %collective-permute-start.27 = (f32[16,1,512]{2,1,0:T(1,128)S(1)}, f32[16,1,512]{2,1,0:T(1,128)S(1)}, u32[]{:S(2)}, u32[]{:S(2)}) collective-permute-start(f32[16,1,512]{2,1,0:T(1,128)S(1)} %get-tuple-element.43), channel_id=1, source_target_pairs={{0,1},{1,2},{2,3},{3,4},{4,5},{5,6},{6,7},{8,9},{9,10},{10,11},{11... | collective-permute-start | bytes 98312 | tf_op jit(solution)/shard_map/ppermute | solution.py:20
  458.9 4.5 collective-permute-start.24
  461.1 5.2 %collective-permute-start.25 = (f32[16,8,1]{2,1,0:T(8,128)S(1)}, f32[16,8,1]{2,1,0:T(8,128)S(1)}, u32[]{:S(2)}, u32[]{:S(2)}) collective-permute-start(f32[16,8,1]{2,1,0:T(8,128)S(1)} %get-tuple-element.41), channel_id=1, source_target_pairs={{0,8},{8,16},{16,24},{24,0},{1,9},{9,17},{17,25},{25,1},{2,10},{10... | collective-permute-start | bytes 1544 | tf_op jit(solution)/shard_map/ppermute | solution.py:20
  467.3 5.2 %collective-permute-start.28 = (f32[16,8,1]{2,1,0:T(8,128)S(1)}, f32[16,8,1]{2,1,0:T(8,128)S(1)}, u32[]{:S(2)}, u32[]{:S(2)}) collective-permute-start(f32[16,8,1]{2,1,0:T(8,128)S(1)} %get-tuple-element.38), channel_id=1, source_target_pairs={{0,8},{8,16},{16,24},{24,0},{1,9},{9,17},{17,25},{25,1},{2,10},{10... | collective-permute-start | bytes 1544 | tf_op jit(solution)/shard_map/ppermute | solution.py:20
  467.8 5.4 %collective-permute-start.29 = (f32[16,8,1]{2,1,0:T(8,128)S(1)}, f32[16,8,1]{2,1,0:T(8,128)S(1)}, u32[]{:S(2)}, u32[]{:S(2)}) collective-permute-start(f32[16,8,1]{2,1,0:T(8,128)S(1)} %get-tuple-element.39), channel_id=1, source_target_pairs={{8,0},{16,8},{24,16},{0,24},{9,1},{17,9},{25,17},{1,25},{10,2},{18... | collective-permute-start | bytes 1544 | tf_op jit(solution)/shard_map/ppermute | solution.py:21
  473.5 5.3 %collective-permute-start.30 = (f32[16,1,514]{2,1,0:T(1,128)S(1)}, f32[16,1,514]{2,1,0:T(1,128)S(1)}, u32[]{:S(2)}, u32[]{:S(2)}) collective-permute-start(f32[16,1,514]{2,1,0:T(1,128)S(1)} %get-tuple-element.26), channel_id=1, source_target_pairs={{0,1},{1,2},{2,3},{3,4},{4,5},{5,6},{6,7},{7,0},{8,9},{9,10},{10,1... | collective-permute-start | bytes 98696 | tf_op jit(solution)/shard_map/ppermute | solution.py:20
  473.6 5.2 %collective-permute-start.31 = (f32[16,1,514]{2,1,0:T(1,128)S(1)}, f32[16,1,514]{2,1,0:T(1,128)S(1)}, u32[]{:S(2)}, u32[]{:S(2)}) collective-permute-start(f32[16,1,514]{2,1,0:T(1,128)S(1)} %get-tuple-element.27), channel_id=1, source_target_pairs={{1,0},{2,1},{3,2},{4,3},{5,4},{6,5},{7,6},{0,7},{9,8},{10,9},{11,1... | collective-permute-start | bytes 98696 | tf_op jit(solution)/shard_map/ppermute | solution.py:21
  479.4 14.4 %copy-start = (f32[16,8,512]{2,1,0:T(8,128)}, f32[16,8,512]{2,1,0:T(8,128)S(1)}, u32[]{:S(2)}) copy-start(f32[16,8,512]{2,1,0:T(8,128)S(1)} %get-tuple-element.11) | copy-start | bytes 786436
  479.4 14.4 %copy-start.1 = (f32[16,8,512]{2,1,0:T(8,128)}, f32[16,8,512]{2,1,0:T(8,128)S(1)}, u32[]{:S(2)}) copy-start(f32[16,8,512]{2,1,0:T(8,128)S(1)} %get-tuple-element.10) | copy-start | bytes 786436
  479.5 11.8 %collective-permute-start.34 = (f32[16,1,512]{2,1,0:T(1,128)S(1)}, f32[16,1,512]{2,1,0:T(1,128)S(1)}, u32[]{:S(2)}, u32[]{:S(2)}) collective-permute-start(f32[16,1,512]{2,1,0:T(1,128)S(1)} %get-tuple-element.36), channel_id=1, source_target_pairs={{1,0},{2,1},{3,2},{4,3},{5,4},{6,5},{7,6},{9,8},{10,9},{11,10},{12... | collective-permute-start | bytes 98312 | tf_op jit(solution)/shard_map/ppermute | solution.py:21
  480.8 10.5 %collective-permute-start.35 = (f32[16,1,512]{2,1,0:T(1,128)S(1)}, f32[16,1,512]{2,1,0:T(1,128)S(1)}, u32[]{:S(2)}, u32[]{:S(2)}) collective-permute-start(f32[16,1,512]{2,1,0:T(1,128)S(1)} %get-tuple-element.37), channel_id=1, source_target_pairs={{0,1},{1,2},{2,3},{3,4},{4,5},{5,6},{6,7},{8,9},{9,10},{10,11},{11... | collective-permute-start | bytes 98312 | tf_op jit(solution)/shard_map/ppermute | solution.py:20
  483.9 4.5 collective-permute-start.32
  486.2 5.2 %collective-permute-start.33 = (f32[16,8,1]{2,1,0:T(8,128)S(1)}, f32[16,8,1]{2,1,0:T(8,128)S(1)}, u32[]{:S(2)}, u32[]{:S(2)}) collective-permute-start(f32[16,8,1]{2,1,0:T(8,128)S(1)} %get-tuple-element.35), channel_id=1, source_target_pairs={{0,8},{8,16},{16,24},{24,0},{1,9},{9,17},{17,25},{25,1},{2,10},{10... | collective-permute-start | bytes 1544 | tf_op jit(solution)/shard_map/ppermute | solution.py:20
where the time goes:
time: 500 us; the launch traced here: 494 us
  matrix products  169 us (34%)
  other arithmetic  136 us (27%)
  starting transfers between devices  99.5 us (20%)
  waiting for transfers between devices  65.2 us (13%)
  local copies, waits for them, and re-layouts  23.2 us (5%)
    dot_general x5, matrix products, filter_circles(): lax.dot_general(spectra, table, (((1,), (1,)), ((), ())), precision=lax.P...  92.3 us
    dot_general x5, matrix products, filter_circles(): spectra = jnp.dot(circles, table, precision=lax.Precision.HIGHEST)  76.2 us
    unnamed x7, other arithmetic  46.9 us
    ppermute x18, starting transfers between devices, extended_2(): after = lax.ppermute(initial, axis, down)  37.2 us
    cos x1, other arithmetic, wave_table(): table = jnp.concatenate([jnp.cos(cos_angles), jnp.sin(sin_angles)], axis=1)  35.4 us
    sin x1, other arithmetic, wave_table(): table = jnp.concatenate([jnp.cos(cos_angles), jnp.sin(sin_angles)], axis=1)  32 us
    ppermute x18, waiting for transfers between devices, extended_2(): after = lax.ppermute(initial, axis, down)  27.7 us
    ppermute x18, waiting for transfers between devices, extended_2(): before = lax.ppermute(last, axis, up)  27.5 us
  transfers between devices with their start and end apart: 46, of which 23 were waited for; matrix products, arithmetic and copies ran while one was open for 63% of the time, Pallas kernels for 0%

commit v1 on v0

--- a/solution.py
+++ b/solution.py
@@ -8,6 +8,18 @@
 ADV_COEF = 0.1
 SOUND = 0.4
 THETA_DIV = 0.3
+
+
+def split_up(array, dim, size):
+    lengths = array.shape
+    tiles = array.reshape(*lengths[:dim], size, lengths[dim] // size, *lengths[dim + 1 :])
+    return jnp.moveaxis(tiles, dim, 0)
+
+
+def laid_out(blocks, dim):
+    blocks = jnp.moveaxis(blocks, 0, dim)
+    shape = blocks.shape
+    return blocks.reshape(*shape[:dim], shape[dim] * shape[dim + 1], *shape[dim + 2 :])
 
 
 def extended_2(array, sides, width, wrap):
@@ -120,7 +132,14 @@
         blocks = stacked[field_index].reshape(lon_count, per_dev, cols_dev)
         circles = lax.all_to_all(blocks, "lon", split_axis=0, concat_axis=2, tiled=True)[0]
         smooth = filter_circles(circles, table, wave_index, item_cut, flagged, circle)
-        returned = lax.all_to_all(smooth[None], "lon", split_axis=2, concat_axis=0, tiled=True)
+        peers, here = (lax.axis_size("lon"), lax.axis_index("lon"))
+        blocks_2 = split_up(smooth[None], 2, peers)
+        finished = [blocks_2[here]]
+        for turn in range(1, peers):
+            sent = blocks_2[here ^ turn]
+            finished.append(lax.ppermute(sent, "lon", [(i_2, i_2 ^ turn) for i_2 in range(peers)]))
+        blocks_2 = jnp.stack(finished)[here ^ jnp.arange(peers)]
+        returned = laid_out(blocks_2, 0)
         results.append(returned.reshape(levels, rows_dev, cols_dev))
     stacked = jnp.stack(results)
     extended = extended_2(stacked, (("lon", 3), ("lat", 2)), 3, True)

time: 500 us -> 429 us (0.86)
  other arithmetic: 136 us -> 80.6 us
  waiting for transfers between devices: 65.2 us -> 53.9 us
  local copies, waits for them, and re-layouts: 23.2 us -> 14.7 us
    unnamed x7 -> x4, other arithmetic: 46.9 us -> 0.01 us
    all_to_all x5 -> x0, starting transfers between devices: 21.9 us -> none  [shards(): lax.all_to_all(smooth[None], 'lon', split_axis=2, concat_axis=0, tiled=True)]
    ppermute x0 -> x15, starting transfers between devices: none -> 20.6 us  [shards(): lax.ppermute(sent, 'lon', [(i_2, i_2 ^ turn) for i_2 in range(peers)])]
    ppermute x18, waiting for transfers between devices: 27.7 us -> 11.6 us  [extended_2(): after = lax.ppermute(initial, axis, down)]
    unnamed x44 -> x78, local copies, waits for them, and re-layouts: 15.4 us -> 6.83 us
    all_to_all x5 -> x0, other arithmetic: 6.86 us -> none  [shards(): lax.all_to_all(smooth[None], 'lon', split_axis=2, concat_axis=0, tiled=True)]
    ppermute x18, waiting for transfers between devices: 27.5 us -> 34.1 us  [extended_2(): before = lax.ppermute(last, axis, up)]
    dot_general x5, matrix products: 76.2 us -> 82.6 us  [filter_circles(): spectra = jnp.dot(circles, table, precision=lax.Precision.HIGHEST)]
  transfers between devices with their start and end apart: 46 -> 56, of which waited for: 23 -> 22; matrix products, arithmetic and copies ran while one was open for 63% -> 60% of each run, Pallas kernels for 0% -> 0%
where the time goes in v1:
time: 429 us; the launch traced here: 424 us
  matrix products  171 us (40%)
  starting transfers between devices  102 us (24%)
  other arithmetic  80.6 us (19%)
  waiting for transfers between devices  53.9 us (13%)
  local copies, waits for them, and re-layouts  14.7 us (3%)
    dot_general x5, matrix products, filter_circles(): lax.dot_general(spectra, table, (((1,), (1,)), ((), ())), precision=lax.P...  88 us
    dot_general x5, matrix products, filter_circles(): spectra = jnp.dot(circles, table, precision=lax.Precision.HIGHEST)  82.6 us
    ppermute x18, starting transfers between devices, extended_2(): after = lax.ppermute(initial, axis, down)  42.8 us
    cos x1, other arithmetic, wave_table(): table = jnp.concatenate([jnp.cos(cos_angles), jnp.sin(sin_angles)], axis=1)  35.4 us
    ppermute x18, waiting for transfers between devices, extended_2(): before = lax.ppermute(last, axis, up)  34.1 us
    sin x1, other arithmetic, wave_table(): table = jnp.concatenate([jnp.cos(cos_angles), jnp.sin(sin_angles)], axis=1)  32 us
    all_to_all x5, starting transfers between devices, shards(): lax.all_to_all(blocks, 'lon', split_axis=0, concat_axis=2, tiled=True)[0]  21.3 us
    ppermute x15, starting transfers between devices, shards(): lax.ppermute(sent, 'lon', [(i_2, i_2 ^ turn) for i_2 in range(peers)])  20.6 us
  transfers between devices with their start and end apart: 56, of which 22 were waited for; matrix products, arithmetic and copies ran while one was open for 60% of the time, Pallas kernels for 0%

profile of v1, /device:TPU:0, one launch (start us, length us, event | category | flops | bytes accessed | tf_op | source)
XLA Modules:
  0.0 423.9 jit_solution(8936031144528728896)
XLA Ops:
  0.6 5.2 %all-to-all-start.3 = ((f32[4,32,512]{2,1,0:T(8,128)}), f32[4,32,512]{2,1,0:T(8,128)S(1)}, u32[]{:S(2)}, u32[]{:S(2)}) async-start(f32[4,32,512]{2,1,0:T(8,128)} %bitcast.245), calls=%async_computation.3 | async-start | bytes 524288 | tf_op jit(solution)/shard_map/all_to_all | solution.py:133
  5.8 35.4 %fusion.3 = f32[2048,1025]{1,0:T(8,128)} fusion(), kind=kLoop, calls=%fused_computation.15 | loop fusion | flops 29388800 | bytes 8396800 | tf_op jit(solution)/shard_map/cos | solution.py:72
  41.7 32.0 %fusion.10 = f32[2048,1023]{1,0:T(8,128)} fusion(s32[1023]{0:T(1024)S(1)} %iota_add_fusion), kind=kLoop, calls=%fused_computation.22 | loop fusion | flops 29331456 | bytes 8384508 | tf_op jit(solution)/shard_map/sin | solution.py:72
  74.5 4.2 all-to-all-start.4
  79.5 4.6 %all-to-all-done.4 = f32[4,32,512]{2,1,0:T(8,128)S(1)} async-done(((f32[4,32,512]{2,1,0:T(8,128)}), f32[4,32,512]{2,1,0:T(8,128)S(1)}, u32[]{:S(2)}, u32[]{:S(2)}) %all-to-all-start.4) | async-done | bytes 262176 | tf_op jit(solution)/shard_map/all_to_all | solution.py:133
  84.1 3.9 all-to-all-start.1
  88.3 17.3 %fusion.22 = f32[32,2048]{1,0:T(8,128)S(1)} fusion(f32[32,2048]{1,0:T(8,128)S(1)} %bitcast.225, f32[2048]{0:T(1024)S(1)} %get-tuple-element.23, s32[2048]{0:T(1024)S(1)} %get-tuple-element.24, s32[32]{0:T(128)S(1)} %select_reduce_fusion, f32[2048,1023]{1,0:T(8,128)} %fusion.10, f32[2048,1025]{1,0:T(8,128)} %fusion.3), kind=kOutput, calls=%fused_computation.45 | convolution fusion | flops 1615003648 | bytes 17318016 | tf_op jit(solution)/shard_map/dot_general | solution.py:78
  105.7 15.5 %fusion.23 = f32[32,2048]{1,0:T(8,128)S(1)} fusion(f32[32,2048]{1,0:T(8,128)S(1)} %bitcast.229, f32[2048]{0:T(1024)} %copy-done, s32[2048]{0:T(1024)} %copy-done.2, s32[32]{0:T(128)} %copy-done.9, f32[2048,1023]{1,0:T(8,128)} %fusion.10, f32[2048,1025]{1,0:T(8,128)S(1)} %bitcast.205), kind=kOutput, calls=%fused_computation.46 | convolution fusion | flops 1615003648 | bytes 17318016 | tf_op jit(solution)/shard_map/dot_general | solution.py:78
  121.2 15.2 %convolution_select_fusion.1 = f32[32,2048]{1,0:T(8,128)S(1)} fusion(f32[32,2048]{1,0:T(8,128)S(1)} %bitcast.226, f32[32,2048]{1,0:T(8,128)S(1)} %fusion.22, pred[32]{0:T(512)(128)(4,1)S(1)} %fusion.94, f32[2048,1023]{1,0:T(8,128)S(1)} %bitcast.211, f32[2048,1025]{1,0:T(8,128)S(1)} %bitcast.205), kind=kOutput, calls=%fused_computation.30 | convolution fusion | flops 1614872576 | bytes 17563680 | tf_op jit(solution)/shard_map/dot_general | solution.py:83
  136.4 15.6 %convolution_select_fusion = f32[32,2048]{1,0:T(8,128)S(1)} fusion(f32[32,2048]{1,0:T(8,128)S(1)} %bitcast.230, f32[32,2048]{1,0:T(8,128)S(1)} %fusion.23, pred[32]{0:T(512)(128)(4,1)S(1)} %fusion.94, f32[2048,1023]{1,0:T(8,128)S(1)} %bitcast.211, f32[2048,1025]{1,0:T(8,128)S(1)} %bitcast.205), kind=kOutput, calls=%fused_computation.27 | convolution fusion | flops 1614872576 | bytes 17563680 | tf_op jit(solution)/shard_map/dot_general | solution.py:83
  153.1 2.1 collective-permute-start.12
  155.2 1.5 collective-permute-start.13
  156.7 3.5 all-to-all-start.2
  160.6 17.3 %fusion.20 = f32[32,2048]{1,0:T(8,128)S(1)} fusion(f32[32,2048]{1,0:T(8,128)S(1)} %bitcast.231, f32[2048]{0:T(1024)S(1)} %copy-done.1, s32[2048]{0:T(1024)S(1)} %copy-done.3, s32[32]{0:T(128)S(1)} %copy-done.10, f32[2048,1023]{1,0:T(8,128)} %fusion.10, f32[2048,1025]{1,0:T(8,128)} %fusion.3), kind=kOutput, calls=%fused_computation.43 | convolution fusion | flops 1615003648 | bytes 17318016 | tf_op jit(solution)/shard_map/dot_general | solution.py:78
  177.9 18.5 %convolution_select_fusion.3 = f32[32,2048]{1,0:T(8,128)S(1)} fusion(f32[32,2048]{1,0:T(8,128)S(1)} %bitcast.232, f32[32,2048]{1,0:T(8,128)S(1)} %fusion.20, pred[32]{0:T(512)(128)(4,1)S(1)} %fusion.94, f32[2048,1023]{1,0:T(8,128)} %fusion.10, f32[2048,1025]{1,0:T(8,128)S(1)} %bitcast.207), kind=kOutput, calls=%fused_computation.36 | convolution fusion | flops 1614872576 | bytes 17563680 | tf_op jit(solution)/shard_map/dot_general | solution.py:83
  196.4 4.6 %all-to-all-start = ((f32[4,32,512]{2,1,0:T(8,128)}), f32[4,32,512]{2,1,0:T(8,128)S(1)}, u32[]{:S(2)}, u32[]{:S(2)}) async-start(f32[4,32,512]{2,1,0:T(8,128)} %bitcast), calls=%async_computation | async-start | bytes 524288 | tf_op jit(solution)/shard_map/all_to_all | solution.py:133
  201.3 15.2 %fusion.21 = f32[32,2048]{1,0:T(8,128)S(1)} fusion(f32[32,2048]{1,0:T(8,128)S(1)} %bitcast.233, f32[2048]{0:T(1024)S(1)} %copy-done.1, s32[2048]{0:T(1024)S(1)} %copy-done.3, s32[32]{0:T(128)S(1)} %copy-done.10, f32[2048,1023]{1,0:T(8,128)} %fusion.10, f32[2048,1025]{1,0:T(8,128)} %fusion.3), kind=kOutput, calls=%fused_computation.44 | convolution fusion | flops 1615003648 | bytes 17318016 | tf_op jit(solution)/shard_map/dot_general | solution.py:78
  216.5 20.1 %convolution_select_fusion.2 = f32[32,2048]{1,0:T(8,128)S(1)} fusion(f32[32,2048]{1,0:T(8,128)S(1)} %bitcast.234, f32[32,2048]{1,0:T(8,128)S(1)} %fusion.21, pred[32]{0:T(512)(128)(4,1)S(1)} %fusion.94, f32[2048,1023]{1,0:T(8,128)} %fusion.10, f32[2048,1025]{1,0:T(8,128)} %fusion.3), kind=kOutput, calls=%fused_computation.33 | convolution fusion | flops 1614872576 | bytes 17563680 | tf_op jit(solution)/shard_map/dot_general | solution.py:83
  237.3 17.3 %fusion.19 = f32[32,2048]{1,0:T(8,128)S(1)} fusion(f32[32,2048]{1,0:T(8,128)S(1)} %bitcast.227, f32[2048]{0:T(1024)S(1)} %copy-done.1, s32[2048]{0:T(1024)S(1)} %copy-done.3, s32[32]{0:T(128)S(1)} %copy-done.10, f32[2048,1023]{1,0:T(8,128)} %fusion.10, f32[2048,1025]{1,0:T(8,128)} %fusion.3), kind=kOutput, calls=%fused_computation.42 | convolution fusion | flops 1615003648 | bytes 17318016 | tf_op jit(solution)/shard_map/dot_general | solution.py:78
  254.6 18.5 %convolution_select_fusion.4 = f32[32,2048]{1,0:T(8,128)S(1)} fusion(f32[32,2048]{1,0:T(8,128)S(1)} %bitcast.228, f32[32,2048]{1,0:T(8,128)S(1)} %fusion.19, pred[32]{0:T(512)(128)(4,1)S(1)} %fusion.94, f32[2048,1023]{1,0:T(8,128)} %fusion.10, f32[2048,1025]{1,0:T(8,128)S(1)} %bitcast.209), kind=kOutput, calls=%fused_computation.39 | convolution fusion | flops 1614872576 | bytes 17563680 | tf_op jit(solution)/shard_map/dot_general | solution.py:83
  273.6 2.1 collective-permute-start
  275.7 1.5 collective-permute-start.1
  279.2 2.9 collective-permute-start.14
  284.6 1.9 collective-permute-start.8
  289.6 1.9 collective-permute-start.5
  293.8 1.9 collective-permute-start.11
  297.1 3.4 collective-permute-done.10
  302.2 2.8 collective-permute-start.16
  305.3 2.9 collective-permute-start.20
  308.2 1.8 collective-permute-done.15
  310.0 3.1 collective-permute-done.16
  313.7 3.5 collective-permute-start.18
  317.4 3.7 collective-permute-start.22
  321.8 8.5 %collective-permute-done.21 = f32[16,1,514]{2,0,1:T(8,128)S(1)} collective-permute-done((f32[16,1,514]{2,0,1:T(8,128)S(1)}, f32[16,1,514]{2,0,1:T(8,128)S(1)}, u32[]{:S(2)}, u32[]{:S(2)}) %collective-permute-start.21) | collective-permute-done | bytes 32928 | tf_op jit(solution)/shard_map/ppermute | solution.py:32
  331.3 4.0 multiply_subtract_fusion
  335.7 1.3 collective-permute-start.25
  337.0 4.5 %collective-permute-start.26 = (f32[16,1,512]{2,0,1:T(8,128)S(1)}, f32[16,1,512]{2,0,1:T(8,128)S(1)}, u32[]{:S(2)}, u32[]{:S(2)}) collective-permute-start(f32[16,1,512]{2,0,1:T(8,128)S(1)} %get-tuple-element.60), channel_id=1, source_target_pairs={{0,1},{1,2},{2,3},{3,4},{4,5},{5,6},{6,7},{8,9},{9,10},{10,11},{11... | collective-permute-start | bytes 98312 | tf_op jit(solution)/shard_map/ppermute | solution.py:32
  342.2 1.5 collective-permute-start.24
  343.7 2.2 collective-permute-done.23
  345.9 2.1 collective-permute-done.24
  348.7 2.7 collective-permute-start.28
  351.4 2.9 collective-permute-done.27
  354.8 3.5 collective-permute-start.30
  358.3 2.2 collective-permute-done.29
  361.0 1.3 collective-permute-start.33
  362.3 3.0 collective-permute-start.34
  365.5 1.6 collective-permute-start.31
  367.5 2.8 collective-permute-done.31
  370.3 2.5 collective-permute-done.32
  373.5 2.6 collective-permute-start.36
  376.1 2.8 collective-permute-done.35
  379.2 3.5 collective-permute-start.38
  382.7 1.9 collective-permute-done.37
  386.4 3.0 collective-permute-start.42
  389.5 2.0 collective-permute-start.39
  391.6 2.5 collective-permute-done.39
  394.1 2.8 collective-permute-done.40
  398.2 2.2 collective-permute-start.44
  400.3 2.3 collective-permute-done.43
  403.1 3.5 collective-permute-start.46
  406.7 1.8 collective-permute-done.45
  410.3 3.0 collective-permute-start.50
  413.4 2.4 collective-permute-start.47
  418.4 2.6 collective-permute-done.48
  (221 shorter events, 35.3 us)
Async XLA Ops:
  0.6 73.9 %all-to-all-start.3 = ((f32[4,32,512]{2,1,0:T(8,128)}), f32[4,32,512]{2,1,0:T(8,128)S(1)}, u32[]{:S(2)}, u32[]{:S(2)}) async-start(f32[4,32,512]{2,1,0:T(8,128)} %bitcast.245), calls=%async_computation.3 | async-start | bytes 524288 | tf_op jit(solution)/shard_map/all_to_all | solution.py:133
  5.8 35.5 %copy-start.7 = (s32[32]{0:T(128)S(1)}, s32[32]{0:T(128)}, u32[]{:S(2)}) copy-start(s32[32]{0:T(128)} %param.14) | copy-start | bytes 388
  5.8 35.7 %copy-start.6 = (s32[32]{0:T(128)S(1)}, s32[32]{0:T(128)}, u32[]{:S(2)}) copy-start(s32[32]{0:T(128)} %param.15) | copy-start | bytes 388
  41.7 37.0 %copy-start.8 = (f32[8]{0:T(128)S(1)}, f32[8]{0:T(128)}, u32[]{:S(2)}) copy-start(f32[8]{0:T(128)} %param.13) | copy-start | bytes 100
  73.8 31.8 %copy-start = (f32[2048]{0:T(1024)}, f32[2048]{0:T(1024)S(1)}, u32[]{:S(2)}) copy-start(f32[2048]{0:T(1024)S(1)} %get-tuple-element.23) | copy-start | bytes 24580
  73.8 31.8 %copy-start.2 = (s32[2048]{0:T(1024)}, s32[2048]{0:T(1024)S(1)}, u32[]{:S(2)}) copy-start(s32[2048]{0:T(1024)S(1)} %get-tuple-element.24) | copy-start | bytes 24580
  74.4 31.2 %copy-start.9 = (s32[32]{0:T(128)}, s32[32]{0:T(128)S(1)}, u32[]{:S(2)}) copy-start(s32[32]{0:T(128)S(1)} %select_reduce_fusion) | copy-start | bytes 388
  74.5 9.6 %all-to-all-start.4 = ((f32[4,32,512]{2,1,0:T(8,128)}), f32[4,32,512]{2,1,0:T(8,128)S(1)}, u32[]{:S(2)}, u32[]{:S(2)}) async-start(f32[4,32,512]{2,1,0:T(8,128)} %bitcast.38), calls=%async_computation.4 | async-start | bytes 524288 | tf_op jit(solution)/shard_map/all_to_all | solution.py:133
  84.1 72.6 %all-to-all-start.1 = ((f32[4,32,512]{2,1,0:T(8,128)}), f32[4,32,512]{2,1,0:T(8,128)S(1)}, u32[]{:S(2)}, u32[]{:S(2)}) async-start(f32[4,32,512]{2,1,0:T(8,128)} %bitcast.11), calls=%async_computation.1 | async-start | bytes 524288 | tf_op jit(solution)/shard_map/all_to_all | solution.py:133
  88.3 32.9 %slice-start.9 = ((s8[8388608]{0:T(1024)(128)(4,1)}), s8[4194304]{0:T(1024)(128)(4,1)S(1)}, s32[]{:S(2)}) async-start(s8[8388608]{0:T(1024)(128)(4,1)} %bitcast.210), calls=%async_computation.14 | async-start | bytes 8388608
  153.1 131.4 %collective-permute-start.12 = (f32[1,32,512]{2,1,0:T(8,128)S(1)}, f32[1,32,512]{2,1,0:T(8,128)}, u32[]{:S(2)}, u32[]{:S(2)}) collective-permute-start(f32[1,32,512]{2,1,0:T(8,128)S(1)} %bitcast.252), channel_id=1, source_target_pairs={{0,8},{8,0},{16,24},{24,16},{1,9},{9,1},{17,25},{25,17},{2,10},{10... | collective-permute-start | bytes 196616 | tf_op jit(solution)/shard_map/ppermute | solution.py:140
  155.2 131.3 %collective-permute-start.13 = (f32[1,32,512]{2,1,0:T(8,128)S(1)}, f32[1,32,512]{2,1,0:T(8,128)}, u32[]{:S(2)}, u32[]{:S(2)}) collective-permute-start(f32[1,32,512]{2,1,0:T(8,128)S(1)} %bitcast.251), channel_id=1, source_target_pairs={{0,16},{8,24},{16,0},{24,8},{1,17},{9,25},{17,1},{25,9},{2,18},{10... | collective-permute-start | bytes 196616 | tf_op jit(solution)/shard_map/ppermute | solution.py:140
  156.7 21.2 %slice-start.3 = ((s8[9437184]{0:T(1024)(128)(4,1)}), s8[1048576]{0:T(1024)(128)(4,1)S(1)}, s32[]{:S(2)}) async-start(s8[9437184]{0:T(1024)(128)(4,1)} %bitcast.206), calls=%async_computation.8 | async-start | bytes 2097152
  156.7 39.7 %all-to-all-start.2 = ((f32[4,32,512]{2,1,0:T(8,128)}), f32[4,32,512]{2,1,0:T(8,128)S(1)}, u32[]{:S(2)}, u32[]{:S(2)}) async-start(f32[4,32,512]{2,1,0:T(8,128)} %bitcast.20), calls=%async_computation.2 | async-start | bytes 524288 | tf_op jit(solution)/shard_map/all_to_all | solution.py:133
  196.4 40.6 %all-to-all-start = ((f32[4,32,512]{2,1,0:T(8,128)}), f32[4,32,512]{2,1,0:T(8,128)S(1)}, u32[]{:S(2)}, u32[]{:S(2)}) async-start(f32[4,32,512]{2,1,0:T(8,128)} %bitcast), calls=%async_computation | async-start | bytes 524288 | tf_op jit(solution)/shard_map/all_to_all | solution.py:133
  273.6 5.6 %collective-permute-start = (f32[1,32,512]{2,1,0:T(8,128)S(1)}, f32[1,32,512]{2,1,0:T(8,128)S(1)}, u32[]{:S(2)}, u32[]{:S(2)}) collective-permute-start(f32[1,32,512]{2,1,0:T(8,128)S(1)} %bitcast.263), channel_id=1, source_target_pairs={{0,8},{8,0},{16,24},{24,16},{1,9},{9,1},{17,25},{25,17},{2,10},{10... | collective-permute-start | bytes 196616 | tf_op jit(solution)/shard_map/ppermute | solution.py:140
  275.7 6.4 %collective-permute-start.1 = (f32[1,32,512]{2,1,0:T(8,128)S(1)}, f32[1,32,512]{2,1,0:T(8,128)S(1)}, u32[]{:S(2)}, u32[]{:S(2)}) collective-permute-start(f32[1,32,512]{2,1,0:T(8,128)S(1)} %bitcast.262), channel_id=1, source_target_pairs={{0,16},{8,24},{16,0},{24,8},{1,17},{9,25},{17,1},{25,9},{2,18},{10... | collective-permute-start | bytes 196616 | tf_op jit(solution)/shard_map/ppermute | solution.py:140
  277.2 5.6 %collective-permute-start.2 = (f32[1,32,512]{2,1,0:T(8,128)S(1)}, f32[1,32,512]{2,1,0:T(8,128)S(1)}, u32[]{:S(2)}, u32[]{:S(2)}) collective-permute-start(f32[1,32,512]{2,1,0:T(8,128)S(1)} %bitcast.261), channel_id=1, source_target_pairs={{0,24},{8,16},{16,8},{24,0},{1,25},{9,17},{17,9},{25,1},{2,26},{10... | collective-permute-start | bytes 196616 | tf_op jit(solution)/shard_map/ppermute | solution.py:140
  279.2 7.9 %collective-permute-start.14 = (f32[1,32,512]{2,1,0:T(8,128)S(1)}, f32[1,32,512]{2,1,0:T(8,128)S(1)}, u32[]{:S(2)}, u32[]{:S(2)}) collective-permute-start(f32[1,32,512]{2,1,0:T(8,128)S(1)} %bitcast.253), channel_id=1, source_target_pairs={{0,24},{8,16},{16,8},{24,0},{1,25},{9,17},{17,9},{25,1},{2,26},{10... | collective-permute-start | bytes 196616 | tf_op jit(solution)/shard_map/ppermute | solution.py:140
  282.1 7.5 %collective-permute-start.6 = (f32[1,32,512]{2,1,0:T(8,128)}, f32[1,32,512]{2,1,0:T(8,128)S(1)}, u32[]{:S(2)}, u32[]{:S(2)}) collective-permute-start(f32[1,32,512]{2,1,0:T(8,128)} %bitcast.194), channel_id=1, source_target_pairs={{0,8},{8,0},{16,24},{24,16},{1,9},{9,1},{17,25},{25,17},{2,10},{10... | collective-permute-start | bytes 196616 | tf_op jit(solution)/shard_map/ppermute | solution.py:140
  282.8 8.7 %collective-permute-start.7 = (f32[1,32,512]{2,1,0:T(8,128)}, f32[1,32,512]{2,1,0:T(8,128)S(1)}, u32[]{:S(2)}, u32[]{:S(2)}) collective-permute-start(f32[1,32,512]{2,1,0:T(8,128)} %bitcast.193), channel_id=1, source_target_pairs={{0,16},{8,24},{16,0},{24,8},{1,17},{9,25},{17,1},{25,9},{2,18},{10... | collective-permute-start | bytes 196616 | tf_op jit(solution)/shard_map/ppermute | solution.py:140
  284.6 7.6 %collective-permute-start.8 = (f32[1,32,512]{2,1,0:T(8,128)S(1)}, f32[1,32,512]{2,1,0:T(8,128)S(1)}, u32[]{:S(2)}, u32[]{:S(2)}) collective-permute-start(f32[1,32,512]{2,1,0:T(8,128)S(1)} %bitcast.260), channel_id=1, source_target_pairs={{0,24},{8,16},{16,8},{24,0},{1,25},{9,17},{17,9},{25,1},{2,26},{10... | collective-permute-start | bytes 196616 | tf_op jit(solution)/shard_map/ppermute | solution.py:140
  286.5 7.3 %collective-permute-start.3 = (f32[1,32,512]{2,1,0:T(8,128)S(1)}, f32[1,32,512]{2,1,0:T(8,128)S(1)}, u32[]{:S(2)}, u32[]{:S(2)}) collective-permute-start(f32[1,32,512]{2,1,0:T(8,128)S(1)} %bitcast.259), channel_id=1, source_target_pairs={{0,8},{8,0},{16,24},{24,16},{1,9},{9,1},{17,25},{25,17},{2,10},{10... | collective-permute-start | bytes 196616 | tf_op jit(solution)/shard_map/ppermute | solution.py:140
  287.1 8.5 %collective-permute-start.4 = (f32[1,32,512]{2,1,0:T(8,128)S(1)}, f32[1,32,512]{2,1,0:T(8,128)S(1)}, u32[]{:S(2)}, u32[]{:S(2)}) collective-permute-start(f32[1,32,512]{2,1,0:T(8,128)S(1)} %bitcast.258), channel_id=1, source_target_pairs={{0,16},{8,24},{16,0},{24,8},{1,17},{9,25},{17,1},{25,9},{2,18},{10... | collective-permute-start | bytes 196616 | tf_op jit(solution)/shard_map/ppermute | solution.py:140
  289.6 6.1 %collective-permute-start.5 = (f32[1,32,512]{2,1,0:T(8,128)S(1)}, f32[1,32,512]{2,1,0:T(8,128)}, u32[]{:S(2)}, u32[]{:S(2)}) collective-permute-start(f32[1,32,512]{2,1,0:T(8,128)S(1)} %bitcast.257), channel_id=1, source_target_pairs={{0,24},{8,16},{16,8},{24,0},{1,25},{9,17},{17,9},{25,1},{2,26},{10... | collective-permute-start | bytes 196616 | tf_op jit(solution)/shard_map/ppermute | solution.py:140
  291.5 5.6 %collective-permute-start.9 = (f32[1,32,512]{2,1,0:T(8,128)S(1)}, f32[1,32,512]{2,1,0:T(8,128)S(1)}, u32[]{:S(2)}, u32[]{:S(2)}) collective-permute-start(f32[1,32,512]{2,1,0:T(8,128)S(1)} %bitcast.256), channel_id=1, source_target_pairs={{0,8},{8,0},{16,24},{24,16},{1,9},{9,1},{17,25},{25,17},{2,10},{10... | collective-permute-start | bytes 196616 | tf_op jit(solution)/shard_map/ppermute | solution.py:140
  292.2 8.4 %collective-permute-start.10 = (f32[1,32,512]{2,1,0:T(8,128)S(1)}, f32[1,32,512]{2,1,0:T(8,128)S(1)}, u32[]{:S(2)}, u32[]{:S(2)}) collective-permute-start(f32[1,32,512]{2,1,0:T(8,128)S(1)} %bitcast.255), channel_id=1, source_target_pairs={{0,16},{8,24},{16,0},{24,8},{1,17},{9,25},{17,1},{25,9},{2,18},{10... | collective-permute-start | bytes 196616 | tf_op jit(solution)/shard_map/ppermute | solution.py:140
  293.8 6.8 %collective-permute-start.11 = (f32[1,32,512]{2,1,0:T(8,128)S(1)}, f32[1,32,512]{2,1,0:T(8,128)S(1)}, u32[]{:S(2)}, u32[]{:S(2)}) collective-permute-start(f32[1,32,512]{2,1,0:T(8,128)S(1)} %bitcast.254), channel_id=1, source_target_pairs={{0,24},{8,16},{16,8},{24,0},{1,25},{9,17},{17,9},{25,1},{2,26},{10... | collective-permute-start | bytes 196616 | tf_op jit(solution)/shard_map/ppermute | solution.py:140
  302.0 8.0 %collective-permute-start.15 = (f32[5,16,8,3]{3,1,2,0:T(8,128)S(1)}, f32[5,16,8,3]{3,1,2,0:T(8,128)S(1)}, u32[]{:S(2)}, u32[]{:S(2)}) collective-permute-start(f32[5,16,8,3]{3,1,2,0:T(8,128)S(1)} %get-tuple-element.29), channel_id=1, source_target_pairs={{0,8},{8,16},{16,24},{24,0},{1,9},{9,17},{17,25},{25,1},{2,10},{10... | collective-permute-start | bytes 23048 | tf_op jit(solution)/shard_map/ppermute | solution.py:32
  302.2 11.0 %collective-permute-start.16 = (f32[5,16,8,3]{3,1,2,0:T(8,128)S(1)}, f32[5,16,8,3]{3,1,2,0:T(8,128)S(1)}, u32[]{:S(2)}, u32[]{:S(2)}) collective-permute-start(f32[5,16,8,3]{3,1,2,0:T(8,128)S(1)} %get-tuple-element.30), channel_id=1, source_target_pairs={{8,0},{16,8},{24,16},{0,24},{9,1},{17,9},{25,17},{1,25},{10,2},{18... | collective-permute-start | bytes 23048 | tf_op jit(solution)/shard_map/ppermute | solution.py:33
  305.3 11.9 %collective-permute-start.19 = (f32[16,8,1]{2,0,1:T(8,128)S(1)}, f32[16,8,1]{2,0,1:T(8,128)S(1)}, u32[]{:S(2)}, u32[]{:S(2)}) collective-permute-start(f32[16,8,1]{2,0,1:T(8,128)S(1)} %get-tuple-element.81), channel_id=1, source_target_pairs={{0,8},{8,16},{16,24},{24,0},{1,9},{9,17},{17,25},{25,1},{2,10},{10... | collective-permute-start | bytes 1544 | tf_op jit(solution)/shard_map/ppermute | solution.py:32
  305.3 11.9 %collective-permute-start.20 = (f32[16,8,1]{2,0,1:T(8,128)S(1)}, f32[16,8,1]{2,0,1:T(8,128)S(1)}, u32[]{:S(2)}, u32[]{:S(2)}) collective-permute-start(f32[16,8,1]{2,0,1:T(8,128)S(1)} %get-tuple-element.82), channel_id=1, source_target_pairs={{8,0},{16,8},{24,16},{0,24},{9,1},{17,9},{25,17},{1,25},{10,2},{18... | collective-permute-start | bytes 1544 | tf_op jit(solution)/shard_map/ppermute | solution.py:33
  313.6 16.9 %collective-permute-start.17 = (f32[5,16,3,518]{3,1,2,0:T(8,128)S(1)}, f32[5,16,3,518]{3,1,2,0:T(8,128)S(1)}, u32[]{:S(2)}, u32[]{:S(2)}) collective-permute-start(f32[5,16,3,518]{3,1,2,0:T(8,128)S(1)} %get-tuple-element.25), channel_id=1, source_target_pairs={{0,1},{1,2},{2,3},{3,4},{4,5},{5,6},{6,7},{7,0},{8,9},{9,10},{10,1... | collective-permute-start | bytes 1491848 | tf_op jit(solution)/shard_map/ppermute | solution.py:32
  313.7 16.9 %collective-permute-start.18 = (f32[5,16,3,518]{3,1,2,0:T(8,128)S(1)}, f32[5,16,3,518]{3,1,2,0:T(8,128)S(1)}, u32[]{:S(2)}, u32[]{:S(2)}) collective-permute-start(f32[5,16,3,518]{3,1,2,0:T(8,128)S(1)} %get-tuple-element.26), channel_id=1, source_target_pairs={{1,0},{2,1},{3,2},{4,3},{5,4},{6,5},{7,6},{0,7},{9,8},{10,9},{11,1... | collective-permute-start | bytes 1491848 | tf_op jit(solution)/shard_map/ppermute | solution.py:33
  317.3 13.0 %collective-permute-start.21 = (f32[16,1,514]{2,0,1:T(8,128)S(1)}, f32[16,1,514]{2,0,1:T(8,128)S(1)}, u32[]{:S(2)}, u32[]{:S(2)}) collective-permute-start(f32[16,1,514]{2,0,1:T(8,128)S(1)} %get-tuple-element.37), channel_id=1, source_target_pairs={{0,1},{1,2},{2,3},{3,4},{4,5},{5,6},{6,7},{7,0},{8,9},{9,10},{10,1... | collective-permute-start | bytes 98696 | tf_op jit(solution)/shard_map/ppermute | solution.py:32
  317.4 13.0 %collective-permute-start.22 = (f32[16,1,514]{2,0,1:T(8,128)S(1)}, f32[16,1,514]{2,0,1:T(8,128)S(1)}, u32[]{:S(2)}, u32[]{:S(2)}) collective-permute-start(f32[16,1,514]{2,0,1:T(8,128)S(1)} %get-tuple-element.38), channel_id=1, source_target_pairs={{1,0},{2,1},{3,2},{4,3},{5,4},{6,5},{7,6},{0,7},{9,8},{10,9},{11,1... | collective-permute-start | bytes 98696 | tf_op jit(solution)/shard_map/ppermute | solution.py:33
  335.7 12.3 %collective-permute-start.25 = (f32[16,1,512]{2,0,1:T(8,128)S(1)}, f32[16,1,512]{2,0,1:T(8,128)S(1)}, u32[]{:S(2)}, u32[]{:S(2)}) collective-permute-start(f32[16,1,512]{2,0,1:T(8,128)S(1)} %get-tuple-element.59), channel_id=1, source_target_pairs={{1,0},{2,1},{3,2},{4,3},{5,4},{6,5},{7,6},{9,8},{10,9},{11,10},{12... | collective-permute-start | bytes 98312 | tf_op jit(solution)/shard_map/ppermute | solution.py:33
  337.0 11.0 %collective-permute-start.26 = (f32[16,1,512]{2,0,1:T(8,128)S(1)}, f32[16,1,512]{2,0,1:T(8,128)S(1)}, u32[]{:S(2)}, u32[]{:S(2)}) collective-permute-start(f32[16,1,512]{2,0,1:T(8,128)S(1)} %get-tuple-element.60), channel_id=1, source_target_pairs={{0,1},{1,2},{2,3},{3,4},{4,5},{5,6},{6,7},{8,9},{9,10},{10,11},{11... | collective-permute-start | bytes 98312 | tf_op jit(solution)/shard_map/ppermute | solution.py:32
  341.6 4.3 %collective-permute-start.23 = (f32[16,8,1]{2,0,1:T(8,128)S(1)}, f32[16,8,1]{2,0,1:T(8,128)S(1)}, u32[]{:S(2)}, u32[]{:S(2)}) collective-permute-start(f32[16,8,1]{2,0,1:T(8,128)S(1)} %get-tuple-element.57), channel_id=1, source_target_pairs={{8,0},{16,8},{24,16},{0,24},{9,1},{17,9},{25,17},{1,25},{10,2},{18... | collective-permute-start | bytes 1544 | tf_op jit(solution)/shard_map/ppermute | solution.py:33
  342.2 5.9 %collective-permute-start.24 = (f32[16,8,1]{2,0,1:T(8,128)S(1)}, f32[16,8,1]{2,0,1:T(8,128)S(1)}, u32[]{:S(2)}, u32[]{:S(2)}) collective-permute-start(f32[16,8,1]{2,0,1:T(8,128)S(1)} %get-tuple-element.58), channel_id=1, source_target_pairs={{0,8},{8,16},{16,24},{24,0},{1,9},{9,17},{17,25},{25,1},{2,10},{10... | collective-permute-start | bytes 1544 | tf_op jit(solution)/shard_map/ppermute | solution.py:32
  348.4 5.8 %collective-permute-start.27 = (f32[16,8,1]{2,0,1:T(8,128)S(1)}, f32[16,8,1]{2,0,1:T(8,128)S(1)}, u32[]{:S(2)}, u32[]{:S(2)}) collective-permute-start(f32[16,8,1]{2,0,1:T(8,128)S(1)} %get-tuple-element.55), channel_id=1, source_target_pairs={{0,8},{8,16},{16,24},{24,0},{1,9},{9,17},{17,25},{25,1},{2,10},{10... | collective-permute-start | bytes 1544 | tf_op jit(solution)/shard_map/ppermute | solution.py:32
  348.7 6.0 %collective-permute-start.28 = (f32[16,8,1]{2,0,1:T(8,128)S(1)}, f32[16,8,1]{2,0,1:T(8,128)S(1)}, u32[]{:S(2)}, u32[]{:S(2)}) collective-permute-start(f32[16,8,1]{2,0,1:T(8,128)S(1)} %get-tuple-element.56), channel_id=1, source_target_pairs={{8,0},{16,8},{24,16},{0,24},{9,1},{17,9},{25,17},{1,25},{10,2},{18... | collective-permute-start | bytes 1544 | tf_op jit(solution)/shard_map/ppermute | solution.py:33
  354.7 5.8 %collective-permute-start.29 = (f32[16,1,514]{2,0,1:T(8,128)S(1)}, f32[16,1,514]{2,0,1:T(8,128)S(1)}, u32[]{:S(2)}, u32[]{:S(2)}) collective-permute-start(f32[16,1,514]{2,0,1:T(8,128)S(1)} %get-tuple-element.35), channel_id=1, source_target_pairs={{0,1},{1,2},{2,3},{3,4},{4,5},{5,6},{6,7},{7,0},{8,9},{9,10},{10,1... | collective-permute-start | bytes 98696 | tf_op jit(solution)/shard_map/ppermute | solution.py:32
  354.8 5.7 %collective-permute-start.30 = (f32[16,1,514]{2,0,1:T(8,128)S(1)}, f32[16,1,514]{2,0,1:T(8,128)S(1)}, u32[]{:S(2)}, u32[]{:S(2)}) collective-permute-start(f32[16,1,514]{2,0,1:T(8,128)S(1)} %get-tuple-element.36), channel_id=1, source_target_pairs={{1,0},{2,1},{3,2},{4,3},{5,4},{6,5},{7,6},{0,7},{9,8},{10,9},{11,1... | collective-permute-start | bytes 98696 | tf_op jit(solution)/shard_map/ppermute | solution.py:33
  361.0 11.8 %collective-permute-start.33 = (f32[16,1,512]{2,0,1:T(8,128)S(1)}, f32[16,1,512]{2,0,1:T(8,128)S(1)}, u32[]{:S(2)}, u32[]{:S(2)}) collective-permute-start(f32[16,1,512]{2,0,1:T(8,128)S(1)} %get-tuple-element.53), channel_id=1, source_target_pairs={{1,0},{2,1},{3,2},{4,3},{5,4},{6,5},{7,6},{9,8},{10,9},{11,10},{12... | collective-permute-start | bytes 98312 | tf_op jit(solution)/shard_map/ppermute | solution.py:33
  362.3 10.5 %collective-permute-start.34 = (f32[16,1,512]{2,0,1:T(8,128)S(1)}, f32[16,1,512]{2,0,1:T(8,128)S(1)}, u32[]{:S(2)}, u32[]{:S(2)}) collective-permute-start(f32[16,1,512]{2,0,1:T(8,128)S(1)} %get-tuple-element.54), channel_id=1, source_target_pairs={{0,1},{1,2},{2,3},{3,4},{4,5},{5,6},{6,7},{8,9},{9,10},{10,11},{11... | collective-permute-start | bytes 98312 | tf_op jit(solution)/shard_map/ppermute | solution.py:32
  365.5 4.9 %collective-permute-start.31 = (f32[16,8,1]{2,0,1:T(8,128)S(1)}, f32[16,8,1]{2,0,1:T(8,128)S(1)}, u32[]{:S(2)}, u32[]{:S(2)}) collective-permute-start(f32[16,8,1]{2,0,1:T(8,128)S(1)} %get-tuple-element.51), channel_id=1, source_target_pairs={{8,0},{16,8},{24,16},{0,24},{9,1},{17,9},{25,17},{1,25},{10,2},{18... | collective-permute-start | bytes 1544 | tf_op jit(solution)/shard_map/ppermute | solution.py:33
  367.0 5.8 %collective-permute-start.32 = (f32[16,8,1]{2,0,1:T(8,128)S(1)}, f32[16,8,1]{2,0,1:T(8,128)S(1)}, u32[]{:S(2)}, u32[]{:S(2)}) collective-permute-start(f32[16,8,1]{2,0,1:T(8,128)S(1)} %get-tuple-element.52), channel_id=1, source_target_pairs={{0,8},{8,16},{16,24},{24,0},{1,9},{9,17},{17,25},{25,1},{2,10},{10... | collective-permute-start | bytes 1544 | tf_op jit(solution)/shard_map/ppermute | solution.py:32
  373.1 5.7 %collective-permute-start.35 = (f32[16,8,1]{2,0,1:T(8,128)S(1)}, f32[16,8,1]{2,0,1:T(8,128)S(1)}, u32[]{:S(2)}, u32[]{:S(2)}) collective-permute-start(f32[16,8,1]{2,0,1:T(8,128)S(1)} %get-tuple-element.49), channel_id=1, source_target_pairs={{0,8},{8,16},{16,24},{24,0},{1,9},{9,17},{17,25},{25,1},{2,10},{10... | collective-permute-start | bytes 1544 | tf_op jit(solution)/shard_map/ppermute | solution.py:32
  373.5 5.6 %collective-permute-start.36 = (f32[16,8,1]{2,0,1:T(8,128)S(1)}, f32[16,8,1]{2,0,1:T(8,128)S(1)}, u32[]{:S(2)}, u32[]{:S(2)}) collective-permute-start(f32[16,8,1]{2,0,1:T(8,128)S(1)} %get-tuple-element.50), channel_id=1, source_target_pairs={{8,0},{16,8},{24,16},{0,24},{9,1},{17,9},{25,17},{1,25},{10,2},{18... | collective-permute-start | bytes 1544 | tf_op jit(solution)/shard_map/ppermute | solution.py:33
  379.1 5.5 %collective-permute-start.37 = (f32[16,1,514]{2,0,1:T(8,128)S(1)}, f32[16,1,514]{2,0,1:T(8,128)S(1)}, u32[]{:S(2)}, u32[]{:S(2)}) collective-permute-start(f32[16,1,514]{2,0,1:T(8,128)S(1)} %get-tuple-element.33), channel_id=1, source_target_pairs={{0,1},{1,2},{2,3},{3,4},{4,5},{5,6},{6,7},{7,0},{8,9},{9,10},{10,1... | collective-permute-start | bytes 98696 | tf_op jit(solution)/shard_map/ppermute | solution.py:32
  379.2 5.4 %collective-permute-start.38 = (f32[16,1,514]{2,0,1:T(8,128)S(1)}, f32[16,1,514]{2,0,1:T(8,128)S(1)}, u32[]{:S(2)}, u32[]{:S(2)}) collective-permute-start(f32[16,1,514]{2,0,1:T(8,128)S(1)} %get-tuple-element.34), channel_id=1, source_target_pairs={{1,0},{2,1},{3,2},{4,3},{5,4},{6,5},{7,6},{0,7},{9,8},{10,9},{11,1... | collective-permute-start | bytes 98696 | tf_op jit(solution)/shard_map/ppermute | solution.py:33
  385.1 11.8 %collective-permute-start.41 = (f32[16,1,512]{2,0,1:T(8,128)S(1)}, f32[16,1,512]{2,0,1:T(8,128)S(1)}, u32[]{:S(2)}, u32[]{:S(2)}) collective-permute-start(f32[16,1,512]{2,0,1:T(8,128)S(1)} %get-tuple-element.47), channel_id=1, source_target_pairs={{1,0},{2,1},{3,2},{4,3},{5,4},{6,5},{7,6},{9,8},{10,9},{11,10},{12... | collective-permute-start | bytes 98312 | tf_op jit(solution)/shard_map/ppermute | solution.py:33
  386.4 10.5 %collective-permute-start.42 = (f32[16,1,512]{2,0,1:T(8,128)S(1)}, f32[16,1,512]{2,0,1:T(8,128)S(1)}, u32[]{:S(2)}, u32[]{:S(2)}) collective-permute-start(f32[16,1,512]{2,0,1:T(8,128)S(1)} %get-tuple-element.48), channel_id=1, source_target_pairs={{0,1},{1,2},{2,3},{3,4},{4,5},{5,6},{6,7},{8,9},{9,10},{10,11},{11... | collective-permute-start | bytes 98312 | tf_op jit(solution)/shard_map/ppermute | solution.py:32
  389.5 4.6 %collective-permute-start.39 = (f32[16,8,1]{2,0,1:T(8,128)S(1)}, f32[16,8,1]{2,0,1:T(8,128)S(1)}, u32[]{:S(2)}, u32[]{:S(2)}) collective-permute-start(f32[16,8,1]{2,0,1:T(8,128)S(1)} %get-tuple-element.45), channel_id=1, source_target_pairs={{8,0},{16,8},{24,16},{0,24},{9,1},{17,9},{25,17},{1,25},{10,2},{18... | collective-permute-start | bytes 1544 | tf_op jit(solution)/shard_map/ppermute | solution.py:33
  391.6 5.3 %collective-permute-start.40 = (f32[16,8,1]{2,0,1:T(8,128)S(1)}, f32[16,8,1]{2,0,1:T(8,128)S(1)}, u32[]{:S(2)}, u32[]{:S(2)}) collective-permute-start(f32[16,8,1]{2,0,1:T(8,128)S(1)} %get-tuple-element.46), channel_id=1, source_target_pairs={{0,8},{8,16},{16,24},{24,0},{1,9},{9,17},{17,25},{25,1},{2,10},{10... | collective-permute-start | bytes 1544 | tf_op jit(solution)/shard_map/ppermute | solution.py:32
  397.4 5.3 %collective-permute-start.43 = (f32[16,8,1]{2,0,1:T(8,128)S(1)}, f32[16,8,1]{2,0,1:T(8,128)S(1)}, u32[]{:S(2)}, u32[]{:S(2)}) collective-permute-start(f32[16,8,1]{2,0,1:T(8,128)S(1)} %get-tuple-element.43), channel_id=1, source_target_pairs={{0,8},{8,16},{16,24},{24,0},{1,9},{9,17},{17,25},{25,1},{2,10},{10... | collective-permute-start | bytes 1544 | tf_op jit(solution)/shard_map/ppermute | solution.py:32
  398.2 4.8 %collective-permute-start.44 = (f32[16,8,1]{2,0,1:T(8,128)S(1)}, f32[16,8,1]{2,0,1:T(8,128)S(1)}, u32[]{:S(2)}, u32[]{:S(2)}) collective-permute-start(f32[16,8,1]{2,0,1:T(8,128)S(1)} %get-tuple-element.44), channel_id=1, source_target_pairs={{8,0},{16,8},{24,16},{0,24},{9,1},{17,9},{25,17},{1,25},{10,2},{18... | collective-permute-start | bytes 1544 | tf_op jit(solution)/shard_map/ppermute | solution.py:33
  403.1 5.4 %collective-permute-start.45 = (f32[16,1,514]{2,0,1:T(8,128)S(1)}, f32[16,1,514]{2,0,1:T(8,128)S(1)}, u32[]{:S(2)}, u32[]{:S(2)}) collective-permute-start(f32[16,1,514]{2,0,1:T(8,128)S(1)} %get-tuple-element.31), channel_id=1, source_target_pairs={{0,1},{1,2},{2,3},{3,4},{4,5},{5,6},{6,7},{7,0},{8,9},{9,10},{10,1... | collective-permute-start | bytes 98696 | tf_op jit(solution)/shard_map/ppermute | solution.py:32
  403.1 5.3 %collective-permute-start.46 = (f32[16,1,514]{2,0,1:T(8,128)S(1)}, f32[16,1,514]{2,0,1:T(8,128)S(1)}, u32[]{:S(2)}, u32[]{:S(2)}) collective-permute-start(f32[16,1,514]{2,0,1:T(8,128)S(1)} %get-tuple-element.32), channel_id=1, source_target_pairs={{1,0},{2,1},{3,2},{4,3},{5,4},{6,5},{7,6},{0,7},{9,8},{10,9},{11,1... | collective-permute-start | bytes 98696 | tf_op jit(solution)/shard_map/ppermute | solution.py:33
  409.0 12.0 %collective-permute-start.49 = (f32[16,1,512]{2,0,1:T(8,128)S(1)}, f32[16,1,512]{2,0,1:T(8,128)S(1)}, u32[]{:S(2)}, u32[]{:S(2)}) collective-permute-start(f32[16,1,512]{2,0,1:T(8,128)S(1)} %get-tuple-element.41), channel_id=1, source_target_pairs={{1,0},{2,1},{3,2},{4,3},{5,4},{6,5},{7,6},{9,8},{10,9},{11,10},{12... | collective-permute-start | bytes 98312 | tf_op jit(solution)/shard_map/ppermute | solution.py:33
  410.3 10.7 %collective-permute-start.50 = (f32[16,1,512]{2,0,1:T(8,128)S(1)}, f32[16,1,512]{2,0,1:T(8,128)S(1)}, u32[]{:S(2)}, u32[]{:S(2)}) collective-permute-start(f32[16,1,512]{2,0,1:T(8,128)S(1)} %get-tuple-element.42), channel_id=1, source_target_pairs={{0,1},{1,2},{2,3},{3,4},{4,5},{5,6},{6,7},{8,9},{9,10},{10,11},{11... | collective-permute-start | bytes 98312 | tf_op jit(solution)/shard_map/ppermute | solution.py:32
  413.4 5.0 %collective-permute-start.47 = (f32[16,8,1]{2,0,1:T(8,128)S(1)}, f32[16,8,1]{2,0,1:T(8,128)S(1)}, u32[]{:S(2)}, u32[]{:S(2)}) collective-permute-start(f32[16,8,1]{2,0,1:T(8,128)S(1)} %get-tuple-element.39), channel_id=1, source_target_pairs={{8,0},{16,8},{24,16},{0,24},{9,1},{17,9},{25,17},{1,25},{10,2},{18... | collective-permute-start | bytes 1544 | tf_op jit(solution)/shard_map/ppermute | solution.py:33
  415.8 5.2 %collective-permute-start.48 = (f32[16,8,1]{2,0,1:T(8,128)S(1)}, f32[16,8,1]{2,0,1:T(8,128)S(1)}, u32[]{:S(2)}, u32[]{:S(2)}) collective-permute-start(f32[16,8,1]{2,0,1:T(8,128)S(1)} %get-tuple-element.40), channel_id=1, source_target_pairs={{0,8},{8,16},{16,24},{24,0},{1,9},{9,17},{17,25},{25,1},{2,10},{10... | collective-permute-start | bytes 1544 | tf_op jit(solution)/shard_map/ppermute | solution.py:32
  (14 other events, 198.3 us)
